TPU v7x, 128 devices: a whole 4x4x4 slice. The times are simulated.
128 devices in a mesh: rep: 16 (over z, y), shard: 8 (over x, core).
Axes of the slice: x: 4, y: 4, z: 4, core: 2. Of those that a mesh axis runs over, the one named last changes fastest.
Arguments:
- grads: bfloat16 [16, 8, 1024, 1024], P('rep', 'shard'), may hold values from -6 to 6
- master: float32 [8, 256, 1024], P('shard'), may hold values from -4 to 4
- moment_one: float32 [8, 256, 1024], P('shard'), may hold values from -4 to 4
- moment_two: float32 [8, 256, 1024], P('shard'), may hold values from 0.01 to 10
- average: float32 [8, 256, 1024], P('shard'), may hold values from -4 to 4
- tensor_owner: int32 [32], replicated, may hold values from 0 to 7, as said below
- tensor_start: int32 [32], replicated, may hold values from 0 to 1008, as said below
- tensor_rows: int32 [32], replicated, may hold values from 16 to 208, as said below
- tensor_slot: int32 [32], replicated, may hold values from 0 to 240, as said below
Outputs:
- new_params: float32 [1024, 1024], replicated
- master_new: float32 [8, 256, 1024], P('shard')
- moment_one_new: float32 [8, 256, 1024], P('shard')
- moment_two_new: float32 [8, 256, 1024], P('shard')
- average_new: float32 [8, 256, 1024], P('shard')
Inputs may be any that keep to these rules, and one draw needn't show every extreme that they name: `tensor_owner`: every owner holds exactly 4 tensors; one owner's tensors have exactly 256 rows together and no owner's more. `tensor_start`: the tensors cover the window's rows without gaps or intersections. `tensor_rows`: each tensor's rows are a multiple of 16. `tensor_slot`: an owner's tensors fill its buffer rows from 0 upward without gaps or intersections.
All inputs are finite; a program needn't handle non-finite values.
Results may differ from a plain program's by a relative error of at most 0.0003.
Values may be sent and summed in bfloat16 or wider, within the bound.
No kernel may reach another device: no remote copies, remote signals or barrier semaphores. Data moves between devices by JAX's collectives and lax.ppermute only.
A program may use at most 128 MiB of HBM per device.

v0:
```python
import math

import jax
import jax.numpy as jnp
from jax import lax
from jax.sharding import PartitionSpec as P

beta_one = 0.9
beta_two = 0.95
epsilon = 1e-08
learn_rate = 0.01
decay_base = 0.1
average_rate = 0.99
step_count = 10.0
reference_batch = 128.0


def optimizer_step(summed, master, moment_one, moment_two, average, decay_scale):
    moment_one_new = beta_one * moment_one + (1.0 - beta_one) * summed
    moment_two_new = beta_two * moment_two + (1.0 - beta_two) * summed * summed
    corr_one = 1.0 - beta_one**step_count
    corr_two = 1.0 - beta_two**step_count
    update = moment_one_new / corr_one / (jnp.sqrt(moment_two_new / corr_two) + epsilon)
    master_new = master * (1.0 - learn_rate * decay_base * decay_scale) - learn_rate * update
    average_new = average_rate * average + (1.0 - average_rate) * master_new
    return (master_new, moment_one_new, moment_two_new, average_new)


def packed_rows(
    gradient, tensor_owner, tensor_start, tensor_rows, tensor_slot, dest_owner, dest_slot, wire_type
):
    slot_begin = tensor_slot[None, :]
    covered = (
        (dest_owner[:, None] == tensor_owner[None, :])
        & (dest_slot[:, None] >= slot_begin)
        & (dest_slot[:, None] < slot_begin + tensor_rows[None, :])
    )
    offset = tensor_start[None, :] + dest_slot[:, None] - slot_begin
    window_row = jnp.sum(jnp.where(covered, offset, 0), axis=1)
    present = jnp.any(covered, axis=1)
    picked = jnp.take(gradient, window_row, axis=0)
    return jnp.where(present[:, None], picked, jnp.zeros((), wire_type))


def add_sources(received):
    return jnp.sum(received, axis=0, dtype=jnp.float32)


def local(
    grads,
    master,
    moment_one,
    moment_two,
    average,
    tensor_owner,
    tensor_start,
    tensor_rows,
    tensor_slot,
):
    gradient = grads[0, 0]
    owners = lax.axis_size("shard")
    replicas = lax.axis_size("rep")
    capacity = master.shape[1]
    row_width = gradient.shape[1]
    row_total = gradient.shape[0]
    decay_scale = math.sqrt(owners * replicas / reference_batch)
    slot_index = jnp.arange(owners * capacity, dtype=jnp.int32)
    dest_owner = slot_index // capacity
    dest_slot = slot_index % capacity
    window_sum = lax.psum(gradient.astype(jnp.float32), "rep")
    packed = packed_rows(
        window_sum,
        tensor_owner,
        tensor_start,
        tensor_rows,
        tensor_slot,
        dest_owner,
        dest_slot,
        jnp.float32,
    )
    packed = packed.reshape(owners, capacity, row_width)
    summed = add_sources(lax.all_to_all(packed, "shard", split_axis=0, concat_axis=0, tiled=True))
    states = optimizer_step(
        summed, master[0], moment_one[0], moment_two[0], average[0], decay_scale
    )
    updated = states[0]
    row_index = jnp.arange(row_total, dtype=jnp.int32)
    inside = (row_index[:, None] >= tensor_start[None, :]) & (
        row_index[:, None] < (tensor_start + tensor_rows)[None, :]
    )
    target = tensor_owner * capacity + tensor_slot - tensor_start
    destination = jnp.sum(jnp.where(inside, target[None, :] + row_index[:, None], 0), axis=1)
    piece = lax.all_gather(updated, "shard", axis=0, tiled=True)
    within = (destination >= 0) & (destination < piece.shape[0])
    picked = jnp.take(piece, jnp.clip(destination, 0, piece.shape[0] - 1), axis=0)
    new_params = jnp.where(within[:, None], picked, jnp.zeros((row_total, row_width), jnp.float32))
    return (new_params, states[0][None], states[1][None], states[2][None], states[3][None])


def solution(mesh):
    in_specs = (
        P("rep", "shard", None, None),
        P("shard", None, None),
        P("shard", None, None),
        P("shard", None, None),
        P("shard", None, None),
        P(),
        P(),
        P(),
        P(),
    )
    out_specs = (
        P(),
        P("shard", None, None),
        P("shard", None, None),
        P("shard", None, None),
        P("shard", None, None),
    )
    return jax.shard_map(local, mesh=mesh, in_specs=in_specs, out_specs=out_specs, check_vma=False)
```

profile of v0, /device:TPU:1, one launch (start us, length us, event | category | flops | bytes accessed | tf_op | source)
XLA Modules:
  0.0 313.1 jit_solution(11101088858374454357)
XLA Ops:
  7.2 0.0 copy-start.3
  7.2 0.0 copy-start.4
  7.2 0.0 copy-start.5
  7.2 0.0 copy-start.2
  7.2 0.0 all-reduce.2.cloned.1.call-start
  7.3 4.1 %bitcast_convert_fusion = f32[1024,1024]{1,0:T(8,128)} fusion(bf16[1,1,1024,1024]{3,2,1,0:T(8,128)(2,1)} %param.9), kind=kLoop, calls=%fused_computation.4 | loop fusion | flops 1048576 | bytes 6291456 | tf_op jit(solution)/shard_map/convert_element_type | solution.py:70
  11.3 0.0 all-reduce.2.cloned.1.call-update
  11.3 0.0 all-gather.2.cloned.1.call-start
  11.5 0.2 select_reduce_fusion
  11.6 0.2 fusion.18
  11.9 106.7 %all-reduce.2.cloned.1.call-done = f32[1024,1024]{1,0:T(8,128)} async-done(((f32[1024,1024]{1,0:T(8,128)}), f32[1024,1024]{1,0:T(8,128)}) %all-reduce.2.cloned.1.call-update) | async-done | bytes 4194320 | tf_op jit(solution)/shard_map/psum | solution.py:70
  118.6 13.9 %gather_fusion = f32[2048,1024]{1,0:T(8,128)} fusion(f32[1024,1024]{1,0:T(8,128)} %all-reduce.2.cloned.1.call-done, s32[2048]{0:T(1024)S(1)} %broadcast_clamp_fusion), kind=kCustom, calls=%fused_computation | custom fusion | bytes 16785408 | tf_op jit(solution)/shard_map/jit(_take)/gather | solution.py:41
  132.4 4.0 %select_select_fusion = f32[8,256,1024]{2,1,0:T(8,128)S(1)} fusion(f32[8,256,1024]{2,1,0:T(8,128)} %bitcast.25, pred[8,256]{1,0:T(8,128)(4,1)S(1)} %compare_and_fusion.1, pred[8,256]{1,0:T(8,128)(4,1)S(1)} %broadcast_in_dim.76), kind=kLoop, calls=%fused_computation.2 | loop fusion | flops 4194304 | bytes 16781312 | tf_op jit(solution)/shard_map/jit(_where)/select_n | solution.py:42
  136.4 100.0 %all_to_all.5 = f32[8,256,1024]{2,1,0:T(8,128)} all-to-all(f32[8,256,1024]{2,1,0:T(8,128)S(1)} %select_select_fusion), channel_id=1, replica_groups=mesh['rep'=16,'shard'=8] {'shard'}, dimensions={0} | all-to-all | bytes 16777216 | tf_op jit(solution)/shard_map/all_to_all | solution.py:82
  236.4 4.5 %reduce_sum.37 = f32[256,1024]{1,0:T(8,128)S(1)} reduce(f32[8,256,1024]{2,1,0:T(8,128)} %all_to_all.5, f32[]{:T(128)} %constant.83.clone.1), dimensions={0}, to_apply=%region_4.5 | reduce | flops 1835008 | bytes 9437188 | tf_op jit(solution)/shard_map/reduce_sum | solution.py:46
  241.0 0.0 copy-done
  241.0 0.0 copy-done.1
  241.0 3.0 fusion.6
  243.9 0.0 all-gather.2.cloned.1.call-update
  244.0 0.1 select_reduce_fusion.1
  244.1 4.2 %multiply_add_fusion = (f32[1,256,1024]{2,1,0:T(8,128)}, f32[1,256,1024]{2,1,0:T(8,128)}, f32[1,256,1024]{2,1,0:T(8,128)}, f32[1,256,1024]{2,1,0:T(8,128)}) fusion(f32[1,256,1024]{2,1,0:T(8,128)} %param.13, f32[1,256,1024]{2,1,0:T(8,128)} %param.10, f32[256,1024]{1,0:T(8,128)S(1)} %reduce_sum.37, f32[1,256,1024]{2,1,0:T(8,128)S(1)} %copy-done.1, ...), kind=kLoop, calls=%fused_computation.19 | loop fusion | flops 4456448 | bytes 9437184 | tf_op jit(solution)/shard_map/add | solution.py:25
  248.4 44.1 %all-gather.2.cloned.1.call-done = f32[2048,1024]{1,0:T(8,128)} async-done(((f32[256,1024]{1,0:T(8,128)}), f32[2048,1024]{1,0:T(8,128)}) %all-gather.2.cloned.1.call-update) | async-done | bytes 8388624 | tf_op jit(solution)/shard_map/all_gather | solution.py:93
  292.4 9.7 %gather_fusion.1 = f32[1024,1024]{1,0:T(8,128)} fusion(f32[2048,1024]{1,0:T(8,128)} %all-gather.2.cloned.1.call-done, s32[1024]{0:T(1024)S(1)} %broadcast_clamp_fusion.1), kind=kCustom, calls=%fused_computation.1 | custom fusion | bytes 8392704 | tf_op jit(solution)/shard_map/jit(_take)/gather | solution.py:95
  302.1 4.2 %select_select_fusion.1 = f32[1024,1024]{1,0:T(8,128)} fusion(f32[1024,1024]{1,0:T(8,128)} %gather_fusion.1, pred[1024]{0:T(1024)(128)(4,1)S(1)} %get-tuple-element.10, pred[1024]{0:T(1024)(128)(4,1)S(1)} %get-tuple-element.9), kind=kLoop, calls=%fused_computation.3 | loop fusion | flops 2097152 | bytes 8390656 | tf_op jit(solution)/shard_map/jit(_where)/select_n | solution.py:96
  (17 shorter events, 0.1 us)
Async XLA Ops:
  7.2 4.2 %copy-start.3 = (s32[32]{0:T(128)S(1)}, s32[32]{0:T(128)}, u32[]{:S(2)}) copy-start(s32[32]{0:T(128)} %param.14) | copy-start | bytes 388
  7.2 4.2 %copy-start.4 = (s32[32]{0:T(128)S(1)}, s32[32]{0:T(128)}, u32[]{:S(2)}) copy-start(s32[32]{0:T(128)} %param.15) | copy-start | bytes 388
  7.2 4.2 %copy-start.5 = (s32[32]{0:T(128)S(1)}, s32[32]{0:T(128)}, u32[]{:S(2)}) copy-start(s32[32]{0:T(128)} %param.16) | copy-start | bytes 388
  7.2 4.2 %copy-start.2 = (s32[32]{0:T(128)S(1)}, s32[32]{0:T(128)}, u32[]{:S(2)}) copy-start(s32[32]{0:T(128)} %param.17) | copy-start | bytes 388
  7.2 111.4 %all-reduce.2.cloned.1.call-start = ((), (), s32[]{:S(2)}) async-start(), calls=%async_computation.1 | async-start | bytes 8388608 | tf_op jit(solution)/shard_map/psum | solution.py:70
  11.3 281.1 %all-gather.2.cloned.1.call-start = ((), (), s32[]{:S(2)}) async-start(), calls=%async_computation.2 | async-start | bytes 9437184 | tf_op jit(solution)/shard_map/all_gather | solution.py:93
  236.4 4.5 %copy-start = (f32[1,256,1024]{2,1,0:T(8,128)S(1)}, f32[1,256,1024]{2,1,0:T(8,128)}, u32[]{:S(2)}) copy-start(f32[1,256,1024]{2,1,0:T(8,128)} %param.12) | copy-start | bytes 3145732
  236.4 4.5 %copy-start.1 = (f32[1,256,1024]{2,1,0:T(8,128)S(1)}, f32[1,256,1024]{2,1,0:T(8,128)}, u32[]{:S(2)}) copy-start(f32[1,256,1024]{2,1,0:T(8,128)} %param.11) | copy-start | bytes 3145732
Sparse Core Ops, SparseCore 0:
  12.0 106.5 all-reduce.1
  244.1 48.2 all-gather.1
where the time goes:
time: 313 us
  waiting for transfers between devices  151 us (48%)
  blocking collectives  100 us (32%)
  other arithmetic  24.4 us (8%)
  local copies, waits for them, and re-layouts  23.6 us (8%)
  between operations  14.2 us (5%)
    psum x1, waiting for transfers between devices, local(): window_sum = lax.psum(gradient.astype(jnp.float32), 'rep')  107 us
    all_to_all x1, blocking collectives, local(): lax.all_to_all(packed, 'shard', split_axis=0, concat_axis=0, tiled=True)  100 us
    all_gather x1, waiting for transfers between devices, local(): piece = lax.all_gather(updated, 'shard', axis=0, tiled=True)  44.1 us
    gather x1, local copies, waits for them, and re-layouts, packed_rows(): picked = jnp.take(gradient, window_row, axis=0)  13.9 us
    gather x1, local copies, waits for them, and re-layouts, local(): jnp.take(piece, jnp.clip(destination, 0, piece.shape[0] - 1), axis=0)  9.71 us
  transfers between devices with their start and end apart: 2, of which 2 were waited for; matrix products, arithmetic and copies ran while one was open for 2% of the time, Pallas kernels for 0%

commit v1 on v0

v1 whole, which is shorter than its diff:
```python
import math

import jax
import jax.numpy as jnp
from jax import lax
from jax.experimental import pallas as pl
from jax.experimental.pallas import tpu as pltpu
from jax.sharding import Mesh, PartitionSpec as P

beta_one = 0.9
beta_two = 0.95
epsilon = 1e-08
learn_rate = 0.01
decay_base = 0.1
average_rate = 0.99
step_count = 10.0
reference_batch = 128.0

REP = ("z", "y")
SHARD = ("x", "core")
ALL = REP + SHARD
N_REP, N_SHARD = 16, 8
UNIT, SUB, LANES = 16, 8, 128
decay_scale = math.sqrt(N_REP * N_SHARD / reference_batch)


def new_master(summed, master, moment_one, moment_two):
    moment_one_new = beta_one * moment_one + (1.0 - beta_one) * summed
    moment_two_new = beta_two * moment_two + (1.0 - beta_two) * summed * summed
    corr_one = 1.0 - beta_one**step_count
    corr_two = 1.0 - beta_two**step_count
    update = moment_one_new / corr_one / (jnp.sqrt(moment_two_new / corr_two) + epsilon)
    master_new = master * (1.0 - learn_rate * decay_base * decay_scale) - learn_rate * update
    return master_new, moment_one_new, moment_two_new


def state_kernel(tiles, master, one, two, average, master_out, one_out, two_out, average_out):
    for unit in range(tiles.shape[1]):
        for half in range(2):
            rows = pl.ds(unit * UNIT + half * SUB, SUB)
            for block in range(N_REP // 2):
                cols = pl.ds(block * LANES, LANES)
                summed = tiles[block * 2 + half, unit]
                m, a, b = new_master(summed, master[rows, cols], one[rows, cols], two[rows, cols])
                master_out[rows, cols] = m
                one_out[rows, cols] = a
                two_out[rows, cols] = b
                average_out[rows, cols] = (
                    average_rate * average[rows, cols] + (1.0 - average_rate) * m
                )


def owner_update(tiles, master, one, two, average):
    rows, width = master.shape
    units = 2
    steps = rows // (units * UNIT)
    block = pl.BlockSpec((units * UNIT, width), lambda s: (s, 0))
    return pl.pallas_call(
        state_kernel,
        grid=(steps,),
        in_specs=[pl.BlockSpec((N_REP, units, SUB, LANES), lambda s: (0, s, 0, 0))] + [block] * 4,
        out_specs=[block] * 4,
        out_shape=[jax.ShapeDtypeStruct((rows, width), jnp.float32)] * 4,
        cost_estimate=pl.CostEstimate(
            flops=20 * rows * width, bytes_accessed=36 * rows * width, transcendentals=rows * width
        ),
        name="owner_update",
    )(tiles, master, one, two, average)


def local(
    grads,
    master,
    moment_one,
    moment_two,
    average,
    tensor_owner,
    tensor_start,
    tensor_rows,
    tensor_slot,
):
    gradient = grads[0, 0]
    row_total, width = gradient.shape
    capacity = master.shape[1]
    blocks = width // LANES
    units = row_total // UNIT
    own_units = units // N_SHARD
    slots = capacity // UNIT
    rep = lax.axis_index(REP)
    shard = lax.axis_index(SHARD)
    col, half = rep // 2, rep % 2

    first = jnp.arange(units, dtype=jnp.int32) * UNIT
    inside = (first[:, None] >= tensor_start[None, :]) & (
        first[:, None] < (tensor_start + tensor_rows)[None, :]
    )
    home = tensor_owner * capacity + tensor_slot - tensor_start
    unit_home = jnp.sum(jnp.where(inside, home[None, :] + first[:, None], 0), axis=1) // UNIT
    slot_first = jnp.arange(slots, dtype=jnp.int32) * UNIT
    held = (
        (tensor_owner[None, :] == shard)
        & (slot_first[:, None] >= tensor_slot[None, :])
        & (slot_first[:, None] < (tensor_slot + tensor_rows)[None, :])
    )
    source = tensor_start - tensor_slot
    slot_unit = jnp.sum(jnp.where(held, source[None, :] + slot_first[:, None], 0), axis=1) // UNIT
    slot_used = jnp.any(held, axis=1)

    def my_tiles(state):
        state = state.reshape(slots, 2, SUB, blocks, LANES)
        return lax.dynamic_slice(
            state, (0, half, 0, col, 0), (slots, 1, SUB, 1, LANES)
        ).reshape(slots, SUB, LANES)

    mine = jnp.stack([my_tiles(s[0]) for s in (master, moment_one, moment_two)], axis=1)
    states = lax.all_gather(mine, SHARD, axis=0, tiled=True)

    packed = gradient.reshape(N_SHARD, own_units, 2, SUB, blocks, LANES)
    packed = packed.transpose(4, 2, 0, 1, 3, 5).reshape(N_REP * N_SHARD, own_units, SUB, LANES)
    received = lax.all_to_all(packed, ALL, split_axis=0, concat_axis=0, tiled=True)
    summed = jnp.sum(received, axis=0, dtype=jnp.float32)

    my_home = lax.dynamic_slice(unit_home, (shard * own_units,), (own_units,))
    picked = jnp.take(states, my_home, axis=0)
    weights, _, _ = new_master(summed, picked[:, 0], picked[:, 1], picked[:, 2])

    spread = jnp.broadcast_to(weights, (N_REP, *weights.shape))
    spread = lax.all_to_all(spread, REP, split_axis=0, concat_axis=0, tiled=True)
    lines = spread.reshape(blocks, 2, own_units, SUB, LANES).transpose(2, 1, 3, 0, 4)
    lines = lines.reshape(own_units * UNIT, width)
    new_params = lax.all_gather(lines, SHARD, axis=0, tiled=True)

    summed, _ = lax.optimization_barrier((summed, lines))
    window = jnp.broadcast_to(summed, (N_SHARD, *summed.shape))
    window = lax.all_to_all(window, SHARD, split_axis=0, concat_axis=0, tiled=True)
    window = window.reshape(units, SUB, LANES)
    own = jnp.take(window, slot_unit, axis=0)
    own = jnp.where(slot_used[:, None, None], own, 0.0)
    tiles = jnp.broadcast_to(own, (N_REP, *own.shape))
    tiles = lax.all_to_all(tiles, REP, split_axis=0, concat_axis=0, tiled=True)
    outs = owner_update(tiles, master[0], moment_one[0], moment_two[0], average[0])
    return (new_params, *(o[None] for o in outs))


def solution(mesh):
    grid = Mesh(mesh.devices.reshape(4, 4, 4, 2), ALL)
    state = P(SHARD, None, None)
    in_specs = (P(REP, SHARD, None, None), state, state, state, state, P(), P(), P(), P())
    out_specs = (P(), state, state, state, state)
    return jax.shard_map(local, mesh=grid, in_specs=in_specs, out_specs=out_specs, check_vma=False)
```

time: 313 us -> 133 us (0.42)
  waiting for transfers between devices: 151 us -> 44.7 us
  blocking collectives: 100 us -> 32.7 us
  other arithmetic: 24.4 us -> 1.89 us
  starting transfers between devices: 0.08 us -> 16.7 us
  local copies, waits for them, and re-layouts: 23.6 us -> 14.6 us
  Pallas kernels: 0 us -> 6.93 us
    psum x1 -> x0, waiting for transfers between devices: 107 us -> none  [local(): window_sum = lax.psum(gradient.astype(jnp.float32), 'rep')]
    all_to_all x1 -> x2, blocking collectives: 100 us -> 32.7 us  [the longest x1 19.5 us: local(): tiles = lax.all_to_all(tiles, REP, split_axis=0, concat_axis=0, tiled=True)]
    all_to_all x0 -> x2, waiting for transfers between devices: none -> 44.7 us  [the longest x1 35.3 us: local(): lax.all_to_all(packed, ALL, split_axis=0, concat_axis=0, tiled=True)]
    all_gather x1 -> x2, waiting for transfers between devices: 44.1 us -> 0.02 us  [the longest x1 0.01 us: local(): states = lax.all_gather(mine, SHARD, axis=0, tiled=True)]
    gather x2, local copies, waits for them, and re-layouts: 23.6 us -> 2.53 us  [the longest x1 1.96 us: local(): picked = jnp.take(states, my_home, axis=0)]
    all_to_all x0 -> x2, starting transfers between devices: none -> 16.7 us  [the longest x1 11.5 us: local(): lax.all_to_all(packed, ALL, split_axis=0, concat_axis=0, tiled=True)]
    select_n x5 -> x4, other arithmetic: 8.17 us -> 0.2 us  [the longest x1 0.1 us: local(): own = jnp.where(slot_used[:, None, None], own, 0.0)]
    pallas_call x0 -> x1, Pallas kernels: none -> 6.93 us  [owner_update(): pl.pallas_call(state_kernel, grid=(steps,), in_specs=[pl.BlockSpec((N_REP...]
  transfers between devices with their start and end apart: 2 -> 4, of which waited for: 2 -> 2; matrix products, arithmetic and copies ran while one was open for 2% -> 5% of each run, Pallas kernels for 0% -> 5%
where the time goes in v1:
time: 133 us; the launch traced here: 132 us
  waiting for transfers between devices  44.7 us (34%)
  blocking collectives  32.7 us (25%)
  starting transfers between devices  16.7 us (13%)
  local copies, waits for them, and re-layouts  14.6 us (11%)
  between operations  14.2 us (11%)
  Pallas kernels  6.93 us (5%)
  other arithmetic  1.89 us (1%)
    all_to_all x1, waiting for transfers between devices, local(): lax.all_to_all(packed, ALL, split_axis=0, concat_axis=0, tiled=True)  35.3 us
    all_to_all x1, blocking collectives, local(): tiles = lax.all_to_all(tiles, REP, split_axis=0, concat_axis=0, tiled=True)  19.5 us
    all_to_all x1, blocking collectives, local(): lax.all_to_all(spread, REP, split_axis=0, concat_axis=0, tiled=True)  13.3 us
    all_to_all x1, starting transfers between devices, local(): lax.all_to_all(packed, ALL, split_axis=0, concat_axis=0, tiled=True)  11.5 us
    all_to_all x1, waiting for transfers between devices, local(): lax.all_to_all(window, SHARD, split_axis=0, concat_axis=0, tiled=True)  9.35 us
    pallas_call x1, Pallas kernels, owner_update(): pl.pallas_call(state_kernel, grid=(steps,), in_specs=[pl.BlockSpec((N_REP...  6.93 us
    unnamed x10, local copies, waits for them, and re-layouts  5.69 us
    all_to_all x1, starting transfers between devices, local(): lax.all_to_all(window, SHARD, split_axis=0, concat_axis=0, tiled=True)  5.16 us
  transfers between devices with their start and end apart: 4, of which 2 were waited for; matrix products, arithmetic and copies ran while one was open for 5% of the time, Pallas kernels for 5%

profile of v1, /device:TPU:1, one launch (start us, length us, event | category | flops | bytes accessed | tf_op | source)
XLA Modules:
  0.0 131.9 jit_solution(17496951698644943404)
XLA Ops:
  7.2 0.9 dynamic-slice_bitcast_fusion.2
  8.1 0.9 dynamic-slice_bitcast_fusion
  9.0 0.7 pad_maximum_fusion
  9.7 3.5 %copy.39 = bf16[8,2,8,8,8,128]{5,4,3,2,1,0:T(8,128)(2,1)} copy(bf16[8,2,8,8,8,128]{5,4,0,1,3,2:T(8,128)(2,1)} %bitcast.91) | data formatting | bytes 4194304 | tf_op jit(solution)/shard_map/transpose | solution.py:119
  13.2 11.5 %all-to-all-start = ((bf16[128,8,8,128]{3,2,1,0:T(8,128)(2,1)}), bf16[128,8,8,128]{3,2,1,0:T(8,128)(2,1)S(1)}, u32[]{:S(2)}, u32[]{:S(2)}) async-start(bf16[128,8,8,128]{3,2,1,0:T(8,128)(2,1)} %bitcast.90), calls=%async_computation | async-start | bytes 4194304 | tf_op jit(solution)/shard_map/all_to_all | solution.py:120
  24.9 0.1 select_reduce_fusion
  25.0 0.1 compare_and_fusion.2
  25.1 35.3 %all-to-all-done = bf16[128,8,8,128]{3,2,1,0:T(8,128)(2,1)S(1)} async-done(((bf16[128,8,8,128]{3,2,1,0:T(8,128)(2,1)}), bf16[128,8,8,128]{3,2,1,0:T(8,128)(2,1)S(1)}, u32[]{:S(2)}, u32[]{:S(2)}) %all-to-all-start) | async-done | bytes 2097184 | tf_op jit(solution)/shard_map/all_to_all | solution.py:120
  60.4 0.4 convert_reduce_fusion
  60.8 2.0 %gather_fusion = f32[8,3,8,128]{3,2,1,0:T(8,128)S(1)} fusion(f32[128,3,8,128]{3,2,1,0:T(8,128)} %all-gather.3.cloned.1.call-done, s32[1024]{0:T(1024)S(1)} %pad_clamp_fusion.1), kind=kCustom, calls=%fused_computation | custom fusion | bytes 196640 | tf_op jit(solution)/shard_map/jit(_take)/gather | solution.py:124
  62.9 13.3 %all_to_all.20 = f32[16,8,8,128]{3,2,1,0:T(8,128)S(1)} all-to-all(f32[16,8,8,128]{3,2,1,0:T(8,128)S(1)} %broadcast_in_dim.81), channel_id=1, replica_groups=mesh['z'=4,'y'=4,'x'=4,'core'=2] {'z','y'}, dimensions={0} | all-to-all | bytes 1048576 | tf_op jit(solution)/shard_map/all_to_all | solution.py:128
  76.2 0.3 copy.40
  76.5 0.9 copy.50
  77.4 0.2 fusion.14
  77.6 0.2 select_reduce_fusion.1
  77.8 0.7 broadcast_in_dim.85
  78.5 5.2 %all-to-all-start.2 = ((f32[8,8,8,128]{3,2,1,0:T(8,128)}), f32[8,8,8,128]{3,2,1,0:T(8,128)S(1)}, u32[]{:S(2)}, u32[]{:S(2)}) async-start(f32[8,8,8,128]{3,2,1,0:T(8,128)} %broadcast_in_dim.85), calls=%async_computation.2 | async-start | bytes 524288 | tf_op jit(solution)/shard_map/all_to_all | solution.py:135
  83.7 9.3 %all-to-all-done.2 = f32[8,8,8,128]{3,2,1,0:T(8,128)S(1)} async-done(((f32[8,8,8,128]{3,2,1,0:T(8,128)}), f32[8,8,8,128]{3,2,1,0:T(8,128)S(1)}, u32[]{:S(2)}, u32[]{:S(2)}) %all-to-all-start.2) | async-done | bytes 262176 | tf_op jit(solution)/shard_map/all_to_all | solution.py:135
  93.1 0.6 gather_fusion.1
  93.7 0.1 select_select_fusion
  93.8 0.1 broadcast_in_dim.88
  93.9 19.5 %all_to_all.21.tiles = f32[16,16,8,128]{3,2,1,0:T(8,128)} all-to-all(f32[16,16,8,128]{3,2,1,0:T(8,128)S(1)} %broadcast_in_dim.88), channel_id=1, replica_groups=mesh['z'=4,'y'=4,'x'=4,'core'=2] {'z','y'}, dimensions={0} | all-to-all | bytes 2097152 | tf_op jit(solution)/shard_map/all_to_all | solution.py:140
  113.3 6.9 %owner_update.1 = (f32[256,1024]{1,0:T(8,128)}, f32[256,1024]{1,0:T(8,128)}, f32[256,1024]{1,0:T(8,128)}, f32[256,1024]{1,0:T(8,128)}) custom-call(f32[16,16,8,128]{3,2,1,0:T(8,128)} %all_to_all.21.tiles, f32[256,1024]{1,0:T(8,128)} %bitcast.100, f32[256,1024]{1,0:T(8,128)} %bitcast.98, f32[256,1024]{1,0:T(8,128)} %bitcast.96, f32[256,1024]{1,0:T(8,128)} %bitcast.101), custom_call_target="tpu_custom_call" | custom-call | flops 5242880 | bytes 9437184 | tf_op jit(solution)/shard_map/owner_update/pallas_call | solution.py:58
  120.3 4.8 %copy.52 = f32[1024,1024]{1,0:T(8,128)} copy(f32[1024,1024]{1,0:T(8,128)} %all-gather.5.cloned.1.call-done) | data formatting | bytes 8388608
  (26 shorter events, 0.4 us)
Async XLA Ops:
  7.2 53.6 %all-gather.3.cloned.1.call-start = ((), (), s32[]{:S(2)}) async-start(), calls=%async_computation.4 | async-start | bytes 1769472 | tf_op jit(solution)/shard_map/all_gather | solution.py:116
  13.2 11.6 %copy-start = (s32[32]{0:T(128)S(1)}, s32[32]{0:T(128)}, u32[]{:S(2)}) copy-start(s32[32]{0:T(128)} %param.17) | copy-start | bytes 388
  13.2 11.6 %copy-start.1 = (s32[32]{0:T(128)S(1)}, s32[32]{0:T(128)}, u32[]{:S(2)}) copy-start(s32[32]{0:T(128)} %param.15) | copy-start | bytes 388
  13.2 11.6 %copy-start.2 = (s32[32]{0:T(128)S(1)}, s32[32]{0:T(128)}, u32[]{:S(2)}) copy-start(s32[32]{0:T(128)} %param.16) | copy-start | bytes 388
  13.2 11.6 %copy-start.3 = (s32[32]{0:T(128)S(1)}, s32[32]{0:T(128)}, u32[]{:S(2)}) copy-start(s32[32]{0:T(128)} %param.14) | copy-start | bytes 388
  13.2 47.2 %all-to-all-start = ((bf16[128,8,8,128]{3,2,1,0:T(8,128)(2,1)}), bf16[128,8,8,128]{3,2,1,0:T(8,128)(2,1)S(1)}, u32[]{:S(2)}, u32[]{:S(2)}) async-start(bf16[128,8,8,128]{3,2,1,0:T(8,128)(2,1)} %bitcast.90), calls=%async_computation | async-start | bytes 4194304 | tf_op jit(solution)/shard_map/all_to_all | solution.py:120
  24.7 95.5 %all-gather.5.cloned.1.call-start = ((), (), s32[]{:S(2)}) async-start(), calls=%async_computation.5 | async-start | bytes 4718592 | tf_op jit(solution)/shard_map/all_gather | solution.py:131
  78.5 14.5 %all-to-all-start.2 = ((f32[8,8,8,128]{3,2,1,0:T(8,128)}), f32[8,8,8,128]{3,2,1,0:T(8,128)S(1)}, u32[]{:S(2)}, u32[]{:S(2)}) async-start(f32[8,8,8,128]{3,2,1,0:T(8,128)} %broadcast_in_dim.85), calls=%async_computation.2 | async-start | bytes 524288 | tf_op jit(solution)/shard_map/all_to_all | solution.py:135
Sparse Core Ops, SparseCore 0:
  10.3 35.7 all-gather.2
  77.5 31.6 all-gather.4

commit v2 on v1

--- a/solution.py
+++ b/solution.py
@@ -27,9 +27,9 @@
 def new_master(summed, master, moment_one, moment_two):
     moment_one_new = beta_one * moment_one + (1.0 - beta_one) * summed
     moment_two_new = beta_two * moment_two + (1.0 - beta_two) * summed * summed
-    corr_one = 1.0 - beta_one**step_count
-    corr_two = 1.0 - beta_two**step_count
-    update = moment_one_new / corr_one / (jnp.sqrt(moment_two_new / corr_two) + epsilon)
+    moment = moment_one_new * (1.0 / (1.0 - beta_one**step_count))
+    spread = jnp.sqrt(moment_two_new * (1.0 / (1.0 - beta_two**step_count)))
+    update = moment / (spread + epsilon)
     master_new = master * (1.0 - learn_rate * decay_base * decay_scale) - learn_rate * update
     return master_new, moment_one_new, moment_two_new
 
@@ -66,6 +66,121 @@
         ),
         name="owner_update",
     )(tiles, master, one, two, average)
+
+
+def place_kernel(where, *refs):
+    pieces, out, sems = refs[:-2], refs[-2], refs[-1]
+    copies = []
+    for n, piece in enumerate(pieces):
+        first = pl.multiple_of(where[n], SUB)
+        copies.append(
+            pltpu.make_async_copy(piece, out.at[pl.ds(first, piece.shape[0])], sems.at[n])
+        )
+    for copy in copies:
+        copy.start()
+    for copy in copies:
+        copy.wait()
+
+
+def place(where, pieces, rows):
+    width = pieces[0].shape[1]
+    return pl.pallas_call(
+        place_kernel,
+        in_specs=[pl.BlockSpec(memory_space=pltpu.SMEM)]
+        + [pl.BlockSpec(memory_space=pltpu.VMEM)] * len(pieces),
+        out_specs=pl.BlockSpec(memory_space=pl.ANY),
+        out_shape=jax.ShapeDtypeStruct((rows, width), jnp.float32),
+        scratch_shapes=[pltpu.SemaphoreType.DMA((len(pieces),))],
+        cost_estimate=pl.CostEstimate(
+            flops=0, bytes_accessed=8 * rows * width, transcendentals=0
+        ),
+        name="place",
+    )(where, *pieces)
+
+
+def arrange_kernel(at, *refs):
+    groups, out = refs[:-1], refs[-1]
+    for far in range(4):
+        y = (at[1] + far) % 4
+        for near in range(4):
+            z = (at[0] + near) % 4
+            cols = pl.ds(pl.multiple_of((z * 2 + y // 2) * LANES, LANES), LANES)
+            for unit in range(groups[far].shape[1]):
+                first = pl.multiple_of(unit * UNIT + y % 2 * SUB, SUB)
+                out[pl.ds(first, SUB), cols] = groups[far][near, unit]
+
+
+def arrange(at, groups):
+    units = groups[0].shape[1]
+    width = N_REP // 2 * LANES
+    return pl.pallas_call(
+        arrange_kernel,
+        in_specs=[pl.BlockSpec(memory_space=pltpu.SMEM)]
+        + [pl.BlockSpec(memory_space=pltpu.VMEM)] * 4,
+        out_specs=pl.BlockSpec(memory_space=pltpu.VMEM),
+        out_shape=jax.ShapeDtypeStruct((units * UNIT, width), jnp.float32),
+        cost_estimate=pl.CostEstimate(
+            flops=0, bytes_accessed=8 * units * UNIT * width, transcendentals=0
+        ),
+        name="arrange",
+    )(at, *groups)
+
+
+def pick_kernel(index, *refs):
+    groups, out, window = refs[:4], refs[4], refs[5]
+    units = groups[0].shape[1]
+    for far in range(4):
+        for core in range(2):
+            for unit in range(units):
+                window[(far * 2 + core) * units + unit] = groups[far][core, unit]
+    for slot in range(out.shape[1]):
+        at = index[slot]
+        tile = window[jnp.maximum(at, 0)]
+        tile = jnp.where(at >= 0, tile, jnp.zeros_like(tile))
+        for copy in range(out.shape[0]):
+            out[copy, slot] = tile
+
+
+def pick(index, groups):
+    units = groups[0].shape[1]
+    slots = index.shape[0]
+    return pl.pallas_call(
+        pick_kernel,
+        in_specs=[pl.BlockSpec(memory_space=pltpu.SMEM)]
+        + [pl.BlockSpec(memory_space=pltpu.VMEM)] * 4,
+        out_specs=pl.BlockSpec(memory_space=pltpu.VMEM),
+        out_shape=jax.ShapeDtypeStruct((N_REP, slots, SUB, LANES), jnp.float32),
+        scratch_shapes=[pltpu.VMEM((8 * units, SUB, LANES), jnp.float32)],
+        cost_estimate=pl.CostEstimate(
+            flops=0, bytes_accessed=4 * N_REP * slots * SUB * LANES, transcendentals=0
+        ),
+        name="pick",
+    )(index, *groups)
+
+
+def shift(array, axis, step):
+    size = 2 if axis == "core" else 4
+    return lax.ppermute(array, axis, [(i, (i + step) % size) for i in range(size)])
+
+
+def gather_lines(lines):
+    rows = lines.shape[0]
+    half = rows // 2
+    x, core = lax.axis_index("x"), lax.axis_index("core")
+    left, right = shift(lines, "x", 1), shift(lines, "x", -1)
+    upper, lower = shift(left[:half], "x", 1), shift(right[half:], "x", -1)
+    pieces, where = [], []
+    for piece, step, offset in (
+        (lines, 0, 0),
+        (left, 3, 0),
+        (right, 1, 0),
+        (upper, 2, 0),
+        (lower, 2, half),
+    ):
+        chip = (x + step) % 4
+        pieces += [piece, shift(piece, "core", 1)]
+        where += [(chip * 2 + core) * rows + offset, (chip * 2 + 1 - core) * rows + offset]
+    return place(jnp.stack(where).astype(jnp.int32), pieces, rows * N_SHARD)
 
 
 def local(
@@ -106,6 +221,11 @@
     slot_unit = jnp.sum(jnp.where(held, source[None, :] + slot_first[:, None], 0), axis=1) // UNIT
     slot_used = jnp.any(held, axis=1)
 
+    packed = gradient.reshape(N_SHARD, own_units, 2, SUB, blocks, LANES)
+    packed = packed.transpose(4, 2, 0, 1, 3, 5).reshape(N_REP * N_SHARD, own_units, SUB, LANES)
+    received = lax.all_to_all(packed, ALL, split_axis=0, concat_axis=0, tiled=True)
+    summed = jnp.sum(received, axis=0, dtype=jnp.float32)
+
     def my_tiles(state):
         state = state.reshape(slots, 2, SUB, blocks, LANES)
         return lax.dynamic_slice(
@@ -113,30 +233,32 @@
         ).reshape(slots, SUB, LANES)
 
     mine = jnp.stack([my_tiles(s[0]) for s in (master, moment_one, moment_two)], axis=1)
-    states = lax.all_gather(mine, SHARD, axis=0, tiled=True)
-
-    packed = gradient.reshape(N_SHARD, own_units, 2, SUB, blocks, LANES)
-    packed = packed.transpose(4, 2, 0, 1, 3, 5).reshape(N_REP * N_SHARD, own_units, SUB, LANES)
-    received = lax.all_to_all(packed, ALL, split_axis=0, concat_axis=0, tiled=True)
-    summed = jnp.sum(received, axis=0, dtype=jnp.float32)
-
-    my_home = lax.dynamic_slice(unit_home, (shard * own_units,), (own_units,))
-    picked = jnp.take(states, my_home, axis=0)
-    weights, _, _ = new_master(summed, picked[:, 0], picked[:, 1], picked[:, 2])
-
-    spread = jnp.broadcast_to(weights, (N_REP, *weights.shape))
-    spread = lax.all_to_all(spread, REP, split_axis=0, concat_axis=0, tiled=True)
-    lines = spread.reshape(blocks, 2, own_units, SUB, LANES).transpose(2, 1, 3, 0, 4)
-    lines = lines.reshape(own_units * UNIT, width)
-    new_params = lax.all_gather(lines, SHARD, axis=0, tiled=True)
-
-    summed, _ = lax.optimization_barrier((summed, lines))
-    window = jnp.broadcast_to(summed, (N_SHARD, *summed.shape))
-    window = lax.all_to_all(window, SHARD, split_axis=0, concat_axis=0, tiled=True)
-    window = window.reshape(units, SUB, LANES)
-    own = jnp.take(window, slot_unit, axis=0)
-    own = jnp.where(slot_used[:, None, None], own, 0.0)
-    tiles = jnp.broadcast_to(own, (N_REP, *own.shape))
+    sent = jnp.take(mine, unit_home % slots, axis=0)
+    sent = jnp.where((unit_home // slots == shard)[:, None, None, None], sent, 0.0)
+    sent = sent.reshape(N_SHARD, own_units, 3, SUB, LANES)
+    sent = sent.reshape(4, 2, own_units, 3, SUB, LANES)
+    x, core = lax.axis_index("x"), lax.axis_index("core")
+    kept = lax.dynamic_index_in_dim(sent, core, axis=1, keepdims=False)
+    given = lax.dynamic_index_in_dim(sent, 1 - core, axis=1, keepdims=False)
+    merged = kept + shift(given, "core", 1)
+    states = lax.dynamic_index_in_dim(merged, x, keepdims=False)
+    for step in (1, 3, 2):
+        piece = lax.dynamic_index_in_dim(merged, (x + step) % 4, keepdims=False)
+        states = states + shift(piece, "x", step)
+
+    weights, _, _ = new_master(summed, states[:, 0], states[:, 1], states[:, 2])
+    z, y = lax.axis_index("z"), lax.axis_index("y")
+    near = jnp.stack([weights] + [shift(weights, "z", step) for step in (3, 2, 1)])
+    far = [near] + [shift(near, "y", step) for step in (3, 2, 1)]
+    lines = arrange(jnp.stack([z, y]).astype(jnp.int32), far)
+    new_params = gather_lines(lines)
+
+    pair = jnp.stack([summed, shift(summed, "core", 1)])
+    window = [pair] + [shift(pair, "x", step) for step in (3, 2, 1)]
+    from_shard = slot_unit // own_units
+    place_of = (from_shard // 2 - x + 4) % 4 * 2 + (from_shard + core) % 2
+    index = place_of * own_units + slot_unit % own_units
+    tiles = pick(jnp.where(slot_used, index, -1).astype(jnp.int32), window)
     tiles = lax.all_to_all(tiles, REP, split_axis=0, concat_axis=0, tiled=True)
     outs = owner_update(tiles, master[0], moment_one[0], moment_two[0], average[0])
     return (new_params, *(o[None] for o in outs))

time: 133 us -> 106 us (0.80)
  blocking collectives: 32.7 us -> 0 us
  starting transfers between devices: 16.7 us -> 48.5 us
  waiting for transfers between devices: 44.7 us -> 25.2 us
  between operations: 14.2 us -> 1.02 us
  Pallas kernels: 6.93 us -> 15.3 us
  local copies, waits for them, and re-layouts: 14.6 us -> 11.9 us
  other arithmetic: 1.89 us -> 3.55 us
    all_to_all x1, waiting for transfers between devices: 35.3 us -> 0.58 us  [local(): lax.all_to_all(packed, ALL, split_axis=0, concat_axis=0, tiled=True)]
    all_to_all x2 -> x0, blocking collectives: 32.7 us -> none  [the longest x1 19.5 us: local(): tiles = lax.all_to_all(tiles, REP, split_axis=0, concat_axis=0, tiled=True)]
    ppermute x0 -> x23, starting transfers between devices: none -> 32.4 us  [shift(): lax.ppermute(array, axis, [(i, (i + step) % size) for i in range(size)])]
    ppermute x0 -> x23, waiting for transfers between devices: none -> 24.6 us  [shift(): lax.ppermute(array, axis, [(i, (i + step) % size) for i in range(size)])]
    all_to_all x1, waiting for transfers between devices: 9.35 us -> 0.01 us  [local(): tiles = lax.all_to_all(tiles, REP, split_axis=0, concat_axis=0, tiled=True)]
    pallas_call x0 -> x3, Pallas kernels: none -> 8.37 us  [the longest x1 4.23 us: place(): pl.pallas_call(place_kernel, in_specs=[pl.BlockSpec(memory_space=pltpu.SM...]
    gather x2 -> x1, local copies, waits for them, and re-layouts: 2.53 us -> 0.65 us  [local(): sent = jnp.take(mine, unit_home % slots, axis=0)]
    unnamed x10 -> x38, local copies, waits for them, and re-layouts: 5.69 us -> 5.14 us
  transfers between devices with their start and end apart: 4 -> 25, of which waited for: 2 -> 7; matrix products, arithmetic and copies ran while one was open for 5% -> 6% of each run, Pallas kernels for 5% -> 10%
where the time goes in v2:
time: 106 us; the launch traced here: 105 us
  starting transfers between devices  48.5 us (46%)
  waiting for transfers between devices  25.2 us (24%)
  Pallas kernels  15.3 us (14%)
  local copies, waits for them, and re-layouts  11.9 us (11%)
  other arithmetic  3.55 us (3%)
    ppermute x23, starting transfers between devices, shift(): lax.ppermute(array, axis, [(i, (i + step) % size) for i in range(size)])  32.4 us
    ppermute x23, waiting for transfers between devices, shift(): lax.ppermute(array, axis, [(i, (i + step) % size) for i in range(size)])  24.6 us
    all_to_all x1, starting transfers between devices, local(): lax.all_to_all(packed, ALL, split_axis=0, concat_axis=0, tiled=True)  11.5 us
    pallas_call x1, Pallas kernels, owner_update(): pl.pallas_call(state_kernel, grid=(steps,), in_specs=[pl.BlockSpec((N_REP...  6.93 us
    unnamed x38, local copies, waits for them, and re-layouts  5.14 us
    all_to_all x1, starting transfers between devices, local(): tiles = lax.all_to_all(tiles, REP, split_axis=0, concat_axis=0, tiled=True)  4.56 us
    pallas_call x1, Pallas kernels, place(): pl.pallas_call(place_kernel, in_specs=[pl.BlockSpec(memory_space=pltpu.SM...  4.23 us
    transpose x1, local copies, waits for them, and re-layouts, local(): packed.transpose(4, 2, 0, 1, 3, 5)  3.51 us
  transfers between devices with their start and end apart: 25, of which 7 were waited for; matrix products, arithmetic and copies ran while one was open for 6% of the time, Pallas kernels for 10%

profile of v2, /device:TPU:1, one launch (start us, length us, event | category | flops | bytes accessed | tf_op | source)
XLA Modules:
  0.0 105.5 jit_solution(4434722567514899812)
XLA Ops:
  0.6 3.5 %copy.25 = bf16[8,2,8,8,8,128]{5,4,3,2,1,0:T(8,128)(2,1)} copy(bf16[8,2,8,8,8,128]{5,4,0,1,3,2:T(8,128)(2,1)} %bitcast.99) | data formatting | bytes 4194304 | tf_op jit(solution)/shard_map/transpose | solution.py:225
  4.2 11.5 %all-to-all-start = ((bf16[128,8,8,128]{3,2,1,0:T(8,128)(2,1)}), bf16[128,8,8,128]{3,2,1,0:T(8,128)(2,1)S(1)}, u32[]{:S(2)}, u32[]{:S(2)}) async-start(bf16[128,8,8,128]{3,2,1,0:T(8,128)(2,1)} %bitcast.97), calls=%async_computation | async-start | bytes 4194304 | tf_op jit(solution)/shard_map/all_to_all | solution.py:226
  19.6 1.1 %collective-permute-start = (f32[4,8,3,8,128]{4,3,2,1,0:T(8,128)S(1)}, f32[4,8,3,8,128]{4,3,2,1,0:T(8,128)S(1)}, u32[]{:S(2)}, u32[]{:S(2)}) collective-permute-start(f32[4,8,3,8,128]{4,3,2,1,0:T(8,128)S(1)} %dynamic-slice_bitcast_fusion), channel_id=1, source_target_pairs={{0,1},{1,0},{2,3},{3,2},{4,5},{5,4},{6,7},{7,6},{8,9},{9,8},{10,11... | collective-permute-start | bytes 1179656 | tf_op jit(solution)/shard_map/ppermute | solution.py:163
  20.9 1.2 %collective-permute-done = f32[4,8,3,8,128]{4,3,2,1,0:T(8,128)S(1)} collective-permute-done((f32[4,8,3,8,128]{4,3,2,1,0:T(8,128)S(1)}, f32[4,8,3,8,128]{4,3,2,1,0:T(8,128)S(1)}, u32[]{:S(2)}, u32[]{:S(2)}) %collective-permute-start) | collective-permute-done | bytes 393248 | tf_op jit(solution)/shard_map/ppermute | solution.py:163
  24.0 2.0 %collective-permute-start.2 = (f32[8,3,8,128]{3,2,0,1:T(8,128)S(1)}, f32[8,3,8,128]{3,2,0,1:T(8,128)S(1)}, u32[]{:S(2)}, u32[]{:S(2)}) collective-permute-start(f32[8,3,8,128]{3,2,0,1:T(8,128)S(1)} %bitcast.109), channel_id=1, source_target_pairs={{0,6},{2,0},{4,2},{6,4},{1,7},{3,1},{5,3},{7,5},{8,14},{10,8},{12,... | collective-permute-start | bytes 294920 | tf_op jit(solution)/shard_map/ppermute | solution.py:163
  27.1 15.8 %collective-permute-done.1 = f32[8,3,8,128]{3,2,0,1:T(8,128)S(1)} collective-permute-done((f32[8,3,8,128]{3,2,0,1:T(8,128)S(1)}, f32[8,3,8,128]{3,2,0,1:T(8,128)S(1)}, u32[]{:S(2)}, u32[]{:S(2)}) %collective-permute-start.1) | collective-permute-done | bytes 98336 | tf_op jit(solution)/shard_map/ppermute | solution.py:163
  43.0 2.4 %collective-permute-done.3 = f32[8,3,8,128]{3,2,0,1:T(8,128)S(1)} collective-permute-done((f32[8,3,8,128]{3,2,0,1:T(8,128)S(1)}, f32[8,3,8,128]{3,2,0,1:T(8,128)S(1)}, u32[]{:S(2)}, u32[]{:S(2)}) %collective-permute-start.3) | collective-permute-done | bytes 98336 | tf_op jit(solution)/shard_map/ppermute | solution.py:163
  47.2 2.9 %collective-permute-start.5 = (f32[8,8,128]{2,1,0:T(8,128)S(1)}, f32[8,8,128]{2,1,0:T(8,128)S(1)}, u32[]{:S(2)}, u32[]{:S(2)}) collective-permute-start(f32[8,8,128]{2,1,0:T(8,128)S(1)} %fusion.15), channel_id=1, source_target_pairs={{0,64},{32,96},{64,0},{96,32},{1,65},{33,97},{65,1},{97,33},{2,66}... | collective-permute-start | bytes 98312 | tf_op jit(solution)/shard_map/ppermute | solution.py:163
  51.1 1.8 %collective-permute-start.19 = (f32[8,8,128]{2,1,0:T(8,128)S(1)}, f32[8,8,128]{2,1,0:T(8,128)S(1)}, u32[]{:S(2)}, u32[]{:S(2)}) collective-permute-start(f32[8,8,128]{2,1,0:T(8,128)S(1)} %convert_reduce_fusion), channel_id=1, source_target_pairs={{0,1},{1,0},{2,3},{3,2},{4,5},{5,4},{6,7},{7,6},{8,9},{9,8},{10,11... | collective-permute-start | bytes 98312 | tf_op jit(solution)/shard_map/ppermute | solution.py:163
  53.2 1.3 %collective-permute-start.9 = (f32[4,8,8,128]{3,2,1,0:T(8,128)S(1)}, f32[4,8,8,128]{3,2,1,0:T(8,128)S(1)}, u32[]{:S(2)}, u32[]{:S(2)}) collective-permute-start(f32[4,8,8,128]{3,2,1,0:T(8,128)S(1)} %pad_maximum_fusion.1.refs_0_), channel_id=1, source_target_pairs={{0,8},{8,16},{16,24},{24,0},{1,9},{9,17},{17,25},{25,1},{2,10},{10... | collective-permute-start | bytes 393224 | tf_op jit(solution)/shard_map/ppermute | solution.py:163
  54.5 2.5 %collective-permute-start.8 = (f32[4,8,8,128]{3,2,1,0:T(8,128)S(1)}, f32[4,8,8,128]{3,2,1,0:T(8,128)S(1)}, u32[]{:S(2)}, u32[]{:S(2)}) collective-permute-start(f32[4,8,8,128]{3,2,1,0:T(8,128)S(1)} %pad_maximum_fusion.1.refs_0_), channel_id=1, source_target_pairs={{0,16},{8,24},{16,0},{24,8},{1,17},{9,25},{17,1},{25,9},{2,18},{10... | collective-permute-start | bytes 393224 | tf_op jit(solution)/shard_map/ppermute | solution.py:163
  59.2 1.8 %collective-permute-start.21 = (f32[2,8,8,128]{3,2,1,0:T(8,128)S(1)}, f32[2,8,8,128]{3,2,1,0:T(8,128)S(1)}, u32[]{:S(2)}, u32[]{:S(2)}) collective-permute-start(f32[2,8,8,128]{3,2,1,0:T(8,128)S(1)} %pad_maximum_fusion.2.refs_0_), channel_id=1, source_target_pairs={{0,4},{2,6},{4,0},{6,2},{1,5},{3,7},{5,1},{7,3},{8,12},{10,14},{12... | collective-permute-start | bytes 196616 | tf_op jit(solution)/shard_map/ppermute | solution.py:163
  63.0 2.1 %arrange.1.refs_0_ = f32[128,1024]{1,0:T(8,128)} custom-call(s32[2]{0:T(128)} %pad_add_fusion.at, f32[4,8,8,128]{3,2,1,0:T(8,128)} %copy-done.6, f32[4,8,8,128]{3,2,1,0:T(8,128)} %copy-done.11, f32[4,8,8,128]{3,2,1,0:T(8,128)} %copy-done.10, f32[4,8,8,128]{3,2,1,0:T(8,128)} %copy-done.9), custom_call_target="tpu_custom_call" | custom-call | bytes 1048576 | tf_op jit(solution)/shard_map/arrange/pallas_call | solution.py:116
  68.5 2.0 %pick.1 = f32[16,16,8,128]{3,2,1,0:T(8,128)} custom-call(s32[16]{0:T(128)} %fusion.22.index, f32[2,8,8,128]{3,2,1,0:T(8,128)} %copy-done.8, f32[2,8,8,128]{3,2,1,0:T(8,128)} %copy-done.14, f32[2,8,8,128]{3,2,1,0:T(8,128)} %copy-done.13, f32[2,8,8,128]{3,2,1,0:T(8,128)} %copy-done.12), custom_call_target="tpu_custom_call" | custom-call | bytes 1048576 | tf_op jit(solution)/shard_map/pick/pallas_call | solution.py:147
  70.5 4.6 %all-to-all-start.1 = ((f32[16,16,8,128]{3,2,1,0:T(8,128)}), f32[16,16,8,128]{3,2,1,0:T(8,128)S(1)}, u32[]{:S(2)}, u32[]{:S(2)}) async-start(f32[16,16,8,128]{3,2,1,0:T(8,128)} %pick.1), calls=%async_computation.1 | async-start | bytes 2097152 | tf_op jit(solution)/shard_map/all_to_all | solution.py:262
  75.1 4.4 %collective-permute-start.10 = (f32[128,1024]{1,0:T(8,128)S(1)}, f32[128,1024]{1,0:T(8,128)S(1)}, u32[]{:S(2)}, u32[]{:S(2)}) collective-permute-start(f32[128,1024]{1,0:T(8,128)S(1)} %copy-done.2), channel_id=1, source_target_pairs={{0,1},{1,0},{2,3},{3,2},{4,5},{5,4},{6,7},{7,6},{8,9},{9,8},{10,11... | collective-permute-start | bytes 1572872 | tf_op jit(solution)/shard_map/ppermute | solution.py:163
  79.6 2.1 %collective-permute-start.17 = (f32[64,1024]{1,0:T(8,128)S(1)}, f32[64,1024]{1,0:T(8,128)S(1)}, u32[]{:S(2)}, u32[]{:S(2)}) collective-permute-start(f32[64,1024]{1,0:T(8,128)S(1)} %slice.26), channel_id=1, source_target_pairs={{0,6},{2,0},{4,2},{6,4},{1,7},{3,1},{5,3},{7,5},{8,14},{10,8},{12,... | collective-permute-start | bytes 786440 | tf_op jit(solution)/shard_map/ppermute | solution.py:163
  81.8 1.3 %collective-permute-start.14 = (f32[128,1024]{1,0:T(8,128)S(1)}, f32[128,1024]{1,0:T(8,128)}, u32[]{:S(2)}, u32[]{:S(2)}) collective-permute-start(f32[128,1024]{1,0:T(8,128)S(1)} %collective-permute-done.13.refs_4_), channel_id=1, source_target_pairs={{0,1},{1,0},{2,3},{3,2},{4,5},{5,4},{6,7},{7,6},{8,9},{9,8},{10,11... | collective-permute-start | bytes 1572872 | tf_op jit(solution)/shard_map/ppermute | solution.py:163
  83.2 3.5 %collective-permute-done.17.refs_8_ = f32[64,1024]{1,0:T(8,128)S(1)} collective-permute-done((f32[64,1024]{1,0:T(8,128)S(1)}, f32[64,1024]{1,0:T(8,128)S(1)}, u32[]{:S(2)}, u32[]{:S(2)}) %collective-permute-start.17) | collective-permute-done | bytes 262176 | tf_op jit(solution)/shard_map/ppermute | solution.py:163
  86.7 1.7 %collective-permute-start.18 = (f32[64,1024]{1,0:T(8,128)S(1)}, f32[64,1024]{1,0:T(8,128)}, u32[]{:S(2)}, u32[]{:S(2)}) collective-permute-start(f32[64,1024]{1,0:T(8,128)S(1)} %collective-permute-done.17.refs_8_), channel_id=1, source_target_pairs={{0,1},{1,0},{2,3},{3,2},{4,5},{5,4},{6,7},{7,6},{8,9},{9,8},{10,11... | collective-permute-start | bytes 786440 | tf_op jit(solution)/shard_map/ppermute | solution.py:163
  88.3 1.4 %collective-permute-done.15.refs_6_ = f32[64,1024]{1,0:T(8,128)} collective-permute-done((f32[64,1024]{1,0:T(8,128)S(1)}, f32[64,1024]{1,0:T(8,128)}, u32[]{:S(2)}, u32[]{:S(2)}) %collective-permute-start.15) | collective-permute-done | bytes 262176 | tf_op jit(solution)/shard_map/ppermute | solution.py:163
  89.7 2.1 %collective-permute-start.16 = (f32[64,1024]{1,0:T(8,128)}, f32[64,1024]{1,0:T(8,128)}, u32[]{:S(2)}, u32[]{:S(2)}) collective-permute-start(f32[64,1024]{1,0:T(8,128)} %collective-permute-done.15.refs_6_), channel_id=1, source_target_pairs={{0,1},{1,0},{2,3},{3,2},{4,5},{5,4},{6,7},{7,6},{8,9},{9,8},{10,11... | collective-permute-start | bytes 786440 | tf_op jit(solution)/shard_map/ppermute | solution.py:163
  93.5 6.9 %owner_update.1 = (f32[256,1024]{1,0:T(8,128)}, f32[256,1024]{1,0:T(8,128)}, f32[256,1024]{1,0:T(8,128)}, f32[256,1024]{1,0:T(8,128)}) custom-call(f32[16,16,8,128]{3,2,1,0:T(8,128)} %copy-done, f32[256,1024]{1,0:T(8,128)} %bitcast.105, f32[256,1024]{1,0:T(8,128)} %bitcast.103, f32[256,1024]{1,0:T(8,128)} %bitcast.101, f32[256,1024]{1,0:T(8,128)} %bitcast.106), custom_call_target="tpu_custom_call" | custom-call | flops 5242880 | bytes 9437184 | tf_op jit(solution)/shard_map/owner_update/pallas_call | solution.py:58
  101.2 4.2 %place.1 = f32[1024,1024]{1,0:T(8,128)} custom-call(s32[10]{0:T(128)} %stack.75.where, f32[128,1024]{1,0:T(8,128)} %arrange.1.refs_0_, f32[128,1024]{1,0:T(8,128)} %copy-done.5, f32[128,1024]{1,0:T(8,128)} %copy-done.4, f32[128,1024]{1,0:T(8,128)} %collective-permute-done.12.refs_3_, f32[128,1024]{1,0:T(8,128)} %copy-done.3, ...), custom_call_target="tpu_custom_call" | custom-call | bytes 8388608 | tf_op jit(solution)/shard_map/place/pallas_call | solution.py:87
  (103 shorter events, 20.2 us)
Async XLA Ops:
  4.2 41.8 %all-to-all-start = ((bf16[128,8,8,128]{3,2,1,0:T(8,128)(2,1)}), bf16[128,8,8,128]{3,2,1,0:T(8,128)(2,1)S(1)}, u32[]{:S(2)}, u32[]{:S(2)}) async-start(bf16[128,8,8,128]{3,2,1,0:T(8,128)(2,1)} %bitcast.97), calls=%async_computation | async-start | bytes 4194304 | tf_op jit(solution)/shard_map/all_to_all | solution.py:226
  23.2 19.7 %collective-permute-start.1 = (f32[8,3,8,128]{3,2,0,1:T(8,128)S(1)}, f32[8,3,8,128]{3,2,0,1:T(8,128)S(1)}, u32[]{:S(2)}, u32[]{:S(2)}) collective-permute-start(f32[8,3,8,128]{3,2,0,1:T(8,128)S(1)} %bitcast.110), channel_id=1, source_target_pairs={{0,2},{2,4},{4,6},{6,0},{1,3},{3,5},{5,7},{7,1},{8,10},{10,12},{12... | collective-permute-start | bytes 294920 | tf_op jit(solution)/shard_map/ppermute | solution.py:163
  24.0 19.0 %collective-permute-start.2 = (f32[8,3,8,128]{3,2,0,1:T(8,128)S(1)}, f32[8,3,8,128]{3,2,0,1:T(8,128)S(1)}, u32[]{:S(2)}, u32[]{:S(2)}) collective-permute-start(f32[8,3,8,128]{3,2,0,1:T(8,128)S(1)} %bitcast.109), channel_id=1, source_target_pairs={{0,6},{2,0},{4,2},{6,4},{1,7},{3,1},{5,3},{7,5},{8,14},{10,8},{12,... | collective-permute-start | bytes 294920 | tf_op jit(solution)/shard_map/ppermute | solution.py:163
  26.0 19.4 %collective-permute-start.3 = (f32[8,3,8,128]{3,2,0,1:T(8,128)S(1)}, f32[8,3,8,128]{3,2,0,1:T(8,128)S(1)}, u32[]{:S(2)}, u32[]{:S(2)}) collective-permute-start(f32[8,3,8,128]{3,2,0,1:T(8,128)S(1)} %bitcast.108), channel_id=1, source_target_pairs={{0,4},{2,6},{4,0},{6,2},{1,5},{3,7},{5,1},{7,3},{8,12},{10,14},{12... | collective-permute-start | bytes 294920 | tf_op jit(solution)/shard_map/ppermute | solution.py:163
  46.4 6.5 %collective-permute-start.6 = (f32[8,8,128]{2,1,0:T(8,128)S(1)}, f32[8,8,128]{2,1,0:T(8,128)S(1)}, u32[]{:S(2)}, u32[]{:S(2)}) collective-permute-start(f32[8,8,128]{2,1,0:T(8,128)S(1)} %fusion.15), channel_id=1, source_target_pairs={{0,32},{32,64},{64,96},{96,0},{1,33},{33,65},{65,97},{97,1},{2,34}... | collective-permute-start | bytes 98312 | tf_op jit(solution)/shard_map/ppermute | solution.py:163
  47.2 5.7 %collective-permute-start.5 = (f32[8,8,128]{2,1,0:T(8,128)S(1)}, f32[8,8,128]{2,1,0:T(8,128)S(1)}, u32[]{:S(2)}, u32[]{:S(2)}) collective-permute-start(f32[8,8,128]{2,1,0:T(8,128)S(1)} %fusion.15), channel_id=1, source_target_pairs={{0,64},{32,96},{64,0},{96,32},{1,65},{33,97},{65,1},{97,33},{2,66}... | collective-permute-start | bytes 98312 | tf_op jit(solution)/shard_map/ppermute | solution.py:163
  50.1 3.1 %collective-permute-start.4 = (f32[8,8,128]{2,1,0:T(8,128)S(1)}, f32[8,8,128]{2,1,0:T(8,128)S(1)}, u32[]{:S(2)}, u32[]{:S(2)}) collective-permute-start(f32[8,8,128]{2,1,0:T(8,128)S(1)} %fusion.15), channel_id=1, source_target_pairs={{0,96},{32,0},{64,32},{96,64},{1,97},{33,1},{65,33},{97,65},{2,98}... | collective-permute-start | bytes 98312 | tf_op jit(solution)/shard_map/ppermute | solution.py:163
  51.1 7.7 %collective-permute-start.19 = (f32[8,8,128]{2,1,0:T(8,128)S(1)}, f32[8,8,128]{2,1,0:T(8,128)S(1)}, u32[]{:S(2)}, u32[]{:S(2)}) collective-permute-start(f32[8,8,128]{2,1,0:T(8,128)S(1)} %convert_reduce_fusion), channel_id=1, source_target_pairs={{0,1},{1,0},{2,3},{3,2},{4,5},{5,4},{6,7},{7,6},{8,9},{9,8},{10,11... | collective-permute-start | bytes 98312 | tf_op jit(solution)/shard_map/ppermute | solution.py:163
  53.2 7.8 %collective-permute-start.9 = (f32[4,8,8,128]{3,2,1,0:T(8,128)S(1)}, f32[4,8,8,128]{3,2,1,0:T(8,128)S(1)}, u32[]{:S(2)}, u32[]{:S(2)}) collective-permute-start(f32[4,8,8,128]{3,2,1,0:T(8,128)S(1)} %pad_maximum_fusion.1.refs_0_), channel_id=1, source_target_pairs={{0,8},{8,16},{16,24},{24,0},{1,9},{9,17},{17,25},{25,1},{2,10},{10... | collective-permute-start | bytes 393224 | tf_op jit(solution)/shard_map/ppermute | solution.py:163
  54.5 7.2 %collective-permute-start.8 = (f32[4,8,8,128]{3,2,1,0:T(8,128)S(1)}, f32[4,8,8,128]{3,2,1,0:T(8,128)S(1)}, u32[]{:S(2)}, u32[]{:S(2)}) collective-permute-start(f32[4,8,8,128]{3,2,1,0:T(8,128)S(1)} %pad_maximum_fusion.1.refs_0_), channel_id=1, source_target_pairs={{0,16},{8,24},{16,0},{24,8},{1,17},{9,25},{17,1},{25,9},{2,18},{10... | collective-permute-start | bytes 393224 | tf_op jit(solution)/shard_map/ppermute | solution.py:163
  57.1 4.7 %collective-permute-start.7 = (f32[4,8,8,128]{3,2,1,0:T(8,128)S(1)}, f32[4,8,8,128]{3,2,1,0:T(8,128)S(1)}, u32[]{:S(2)}, u32[]{:S(2)}) collective-permute-start(f32[4,8,8,128]{3,2,1,0:T(8,128)S(1)} %pad_maximum_fusion.1.refs_0_), channel_id=1, source_target_pairs={{0,24},{8,0},{16,8},{24,16},{1,25},{9,1},{17,9},{25,17},{2,26},{10... | collective-permute-start | bytes 393224 | tf_op jit(solution)/shard_map/ppermute | solution.py:163
  58.8 8.4 %collective-permute-start.22 = (f32[2,8,8,128]{3,2,1,0:T(8,128)S(1)}, f32[2,8,8,128]{3,2,1,0:T(8,128)S(1)}, u32[]{:S(2)}, u32[]{:S(2)}) collective-permute-start(f32[2,8,8,128]{3,2,1,0:T(8,128)S(1)} %pad_maximum_fusion.2.refs_0_), channel_id=1, source_target_pairs={{0,2},{2,4},{4,6},{6,0},{1,3},{3,5},{5,7},{7,1},{8,10},{10,12},{12... | collective-permute-start | bytes 196616 | tf_op jit(solution)/shard_map/ppermute | solution.py:163
  59.2 8.0 %collective-permute-start.21 = (f32[2,8,8,128]{3,2,1,0:T(8,128)S(1)}, f32[2,8,8,128]{3,2,1,0:T(8,128)S(1)}, u32[]{:S(2)}, u32[]{:S(2)}) collective-permute-start(f32[2,8,8,128]{3,2,1,0:T(8,128)S(1)} %pad_maximum_fusion.2.refs_0_), channel_id=1, source_target_pairs={{0,4},{2,6},{4,0},{6,2},{1,5},{3,7},{5,1},{7,3},{8,12},{10,14},{12... | collective-permute-start | bytes 196616 | tf_op jit(solution)/shard_map/ppermute | solution.py:163
  61.0 6.3 %collective-permute-start.20 = (f32[2,8,8,128]{3,2,1,0:T(8,128)S(1)}, f32[2,8,8,128]{3,2,1,0:T(8,128)S(1)}, u32[]{:S(2)}, u32[]{:S(2)}) collective-permute-start(f32[2,8,8,128]{3,2,1,0:T(8,128)S(1)} %pad_maximum_fusion.2.refs_0_), channel_id=1, source_target_pairs={{0,6},{2,0},{4,2},{6,4},{1,7},{3,1},{5,3},{7,5},{8,14},{10,8},{12,... | collective-permute-start | bytes 196616 | tf_op jit(solution)/shard_map/ppermute | solution.py:163
  65.1 14.4 %collective-permute-start.13 = (f32[128,1024]{1,0:T(8,128)}, f32[128,1024]{1,0:T(8,128)S(1)}, u32[]{:S(2)}, u32[]{:S(2)}) collective-permute-start(f32[128,1024]{1,0:T(8,128)} %arrange.1.refs_0_), channel_id=1, source_target_pairs={{0,6},{2,0},{4,2},{6,4},{1,7},{3,1},{5,3},{7,5},{8,14},{10,8},{12,... | collective-permute-start | bytes 1572872 | tf_op jit(solution)/shard_map/ppermute | solution.py:163
  65.9 15.8 %collective-permute-start.11 = (f32[128,1024]{1,0:T(8,128)}, f32[128,1024]{1,0:T(8,128)S(1)}, u32[]{:S(2)}, u32[]{:S(2)}) collective-permute-start(f32[128,1024]{1,0:T(8,128)} %arrange.1.refs_0_), channel_id=1, source_target_pairs={{0,2},{2,4},{4,6},{6,0},{1,3},{3,5},{5,7},{7,1},{8,10},{10,12},{12... | collective-permute-start | bytes 1572872 | tf_op jit(solution)/shard_map/ppermute | solution.py:163
  70.5 22.0 %all-to-all-start.1 = ((f32[16,16,8,128]{3,2,1,0:T(8,128)}), f32[16,16,8,128]{3,2,1,0:T(8,128)S(1)}, u32[]{:S(2)}, u32[]{:S(2)}) async-start(f32[16,16,8,128]{3,2,1,0:T(8,128)} %pick.1), calls=%async_computation.1 | async-start | bytes 2097152 | tf_op jit(solution)/shard_map/all_to_all | solution.py:262
  75.1 25.3 %collective-permute-start.10 = (f32[128,1024]{1,0:T(8,128)S(1)}, f32[128,1024]{1,0:T(8,128)S(1)}, u32[]{:S(2)}, u32[]{:S(2)}) collective-permute-start(f32[128,1024]{1,0:T(8,128)S(1)} %copy-done.2), channel_id=1, source_target_pairs={{0,1},{1,0},{2,3},{3,2},{4,5},{5,4},{6,7},{7,6},{8,9},{9,8},{10,11... | collective-permute-start | bytes 1572872 | tf_op jit(solution)/shard_map/ppermute | solution.py:163
  79.6 7.1 %collective-permute-start.17 = (f32[64,1024]{1,0:T(8,128)S(1)}, f32[64,1024]{1,0:T(8,128)S(1)}, u32[]{:S(2)}, u32[]{:S(2)}) collective-permute-start(f32[64,1024]{1,0:T(8,128)S(1)} %slice.26), channel_id=1, source_target_pairs={{0,6},{2,0},{4,2},{6,4},{1,7},{3,1},{5,3},{7,5},{8,14},{10,8},{12,... | collective-permute-start | bytes 786440 | tf_op jit(solution)/shard_map/ppermute | solution.py:163
  81.7 8.0 %collective-permute-start.15 = (f32[64,1024]{1,0:T(8,128)S(1)}, f32[64,1024]{1,0:T(8,128)}, u32[]{:S(2)}, u32[]{:S(2)}) collective-permute-start(f32[64,1024]{1,0:T(8,128)S(1)} %slice.25), channel_id=1, source_target_pairs={{0,2},{2,4},{4,6},{6,0},{1,3},{3,5},{5,7},{7,1},{8,10},{10,12},{12... | collective-permute-start | bytes 786440 | tf_op jit(solution)/shard_map/ppermute | solution.py:163
  81.8 18.7 %collective-permute-start.14 = (f32[128,1024]{1,0:T(8,128)S(1)}, f32[128,1024]{1,0:T(8,128)}, u32[]{:S(2)}, u32[]{:S(2)}) collective-permute-start(f32[128,1024]{1,0:T(8,128)S(1)} %collective-permute-done.13.refs_4_), channel_id=1, source_target_pairs={{0,1},{1,0},{2,3},{3,2},{4,5},{5,4},{6,7},{7,6},{8,9},{9,8},{10,11... | collective-permute-start | bytes 1572872 | tf_op jit(solution)/shard_map/ppermute | solution.py:163
  83.1 17.4 %collective-permute-start.12 = (f32[128,1024]{1,0:T(8,128)S(1)}, f32[128,1024]{1,0:T(8,128)}, u32[]{:S(2)}, u32[]{:S(2)}) collective-permute-start(f32[128,1024]{1,0:T(8,128)S(1)} %collective-permute-done.11.refs_2_), channel_id=1, source_target_pairs={{0,1},{1,0},{2,3},{3,2},{4,5},{5,4},{6,7},{7,6},{8,9},{9,8},{10,11... | collective-permute-start | bytes 1572872 | tf_op jit(solution)/shard_map/ppermute | solution.py:163
  86.7 13.8 %collective-permute-start.18 = (f32[64,1024]{1,0:T(8,128)S(1)}, f32[64,1024]{1,0:T(8,128)}, u32[]{:S(2)}, u32[]{:S(2)}) collective-permute-start(f32[64,1024]{1,0:T(8,128)S(1)} %collective-permute-done.17.refs_8_), channel_id=1, source_target_pairs={{0,1},{1,0},{2,3},{3,2},{4,5},{5,4},{6,7},{7,6},{8,9},{9,8},{10,11... | collective-permute-start | bytes 786440 | tf_op jit(solution)/shard_map/ppermute | solution.py:163
  89.7 10.8 %collective-permute-start.16 = (f32[64,1024]{1,0:T(8,128)}, f32[64,1024]{1,0:T(8,128)}, u32[]{:S(2)}, u32[]{:S(2)}) collective-permute-start(f32[64,1024]{1,0:T(8,128)} %collective-permute-done.15.refs_6_), channel_id=1, source_target_pairs={{0,1},{1,0},{2,3},{3,2},{4,5},{5,4},{6,7},{7,6},{8,9},{9,8},{10,11... | collective-permute-start | bytes 786440 | tf_op jit(solution)/shard_map/ppermute | solution.py:163
  (20 other events, 135.7 us)

commit v3 on v2

--- a/solution.py
+++ b/solution.py
@@ -1,3 +1,4 @@
+import functools
 import math
 
 import jax
@@ -52,7 +53,7 @@
 
 def owner_update(tiles, master, one, two, average):
     rows, width = master.shape
-    units = 2
+    units = 8
     steps = rows // (units * UNIT)
     block = pl.BlockSpec((units * UNIT, width), lambda s: (s, 0))
     return pl.pallas_call(
@@ -68,8 +69,8 @@
     )(tiles, master, one, two, average)
 
 
-def place_kernel(where, *refs):
-    pieces, out, sems = refs[:-2], refs[-2], refs[-1]
+def place_kernel(count, where, *refs):
+    pieces, out, sems = refs[:count], refs[-2], refs[-1]
     copies = []
     for n, piece in enumerate(pieces):
         first = pl.multiple_of(where[n], SUB)
@@ -82,20 +83,24 @@
         copy.wait()
 
 
-def place(where, pieces, rows):
-    width = pieces[0].shape[1]
-    return pl.pallas_call(
-        place_kernel,
+def place(where, pieces, rows, held=None):
+    width, count = pieces[0].shape[1], len(pieces)
+    given = [] if held is None else [held]
+    return pl.pallas_call(
+        functools.partial(place_kernel, count),
         in_specs=[pl.BlockSpec(memory_space=pltpu.SMEM)]
-        + [pl.BlockSpec(memory_space=pltpu.VMEM)] * len(pieces),
+        + [pl.BlockSpec(memory_space=pltpu.VMEM)] * count
+        + [pl.BlockSpec(memory_space=pl.ANY)] * len(given),
         out_specs=pl.BlockSpec(memory_space=pl.ANY),
         out_shape=jax.ShapeDtypeStruct((rows, width), jnp.float32),
-        scratch_shapes=[pltpu.SemaphoreType.DMA((len(pieces),))],
-        cost_estimate=pl.CostEstimate(
-            flops=0, bytes_accessed=8 * rows * width, transcendentals=0
+        scratch_shapes=[pltpu.SemaphoreType.DMA((count,))],
+        input_output_aliases={} if held is None else {count + 1: 0},
+        compiler_params=pltpu.CompilerParams(vmem_limit_bytes=6 << 20),
+        cost_estimate=pl.CostEstimate(
+            flops=0, bytes_accessed=8 * width * sum(p.shape[0] for p in pieces), transcendentals=0
         ),
         name="place",
-    )(where, *pieces)
+    )(jnp.stack(where).astype(jnp.int32), *pieces, *given)
 
 
 def arrange_kernel(at, *refs):
@@ -119,6 +124,7 @@
         + [pl.BlockSpec(memory_space=pltpu.VMEM)] * 4,
         out_specs=pl.BlockSpec(memory_space=pltpu.VMEM),
         out_shape=jax.ShapeDtypeStruct((units * UNIT, width), jnp.float32),
+        compiler_params=pltpu.CompilerParams(vmem_limit_bytes=4 << 20),
         cost_estimate=pl.CostEstimate(
             flops=0, bytes_accessed=8 * units * UNIT * width, transcendentals=0
         ),
@@ -151,6 +157,7 @@
         out_specs=pl.BlockSpec(memory_space=pltpu.VMEM),
         out_shape=jax.ShapeDtypeStruct((N_REP, slots, SUB, LANES), jnp.float32),
         scratch_shapes=[pltpu.VMEM((8 * units, SUB, LANES), jnp.float32)],
+        compiler_params=pltpu.CompilerParams(vmem_limit_bytes=4 << 20),
         cost_estimate=pl.CostEstimate(
             flops=0, bytes_accessed=4 * N_REP * slots * SUB * LANES, transcendentals=0
         ),
@@ -169,18 +176,18 @@
     x, core = lax.axis_index("x"), lax.axis_index("core")
     left, right = shift(lines, "x", 1), shift(lines, "x", -1)
     upper, lower = shift(left[:half], "x", 1), shift(right[half:], "x", -1)
-    pieces, where = [], []
-    for piece, step, offset in (
-        (lines, 0, 0),
-        (left, 3, 0),
-        (right, 1, 0),
-        (upper, 2, 0),
-        (lower, 2, half),
+    out = None
+    for group in (
+        ((lines, 0, 0), (left, 3, 0), (right, 1, 0)),
+        ((upper, 2, 0), (lower, 2, half)),
     ):
-        chip = (x + step) % 4
-        pieces += [piece, shift(piece, "core", 1)]
-        where += [(chip * 2 + core) * rows + offset, (chip * 2 + 1 - core) * rows + offset]
-    return place(jnp.stack(where).astype(jnp.int32), pieces, rows * N_SHARD)
+        pieces, where = [], []
+        for piece, step, offset in group:
+            chip = (x + step) % 4
+            pieces += [piece, shift(piece, "core", 1)]
+            where += [(chip * 2 + core) * rows + offset, (chip * 2 + 1 - core) * rows + offset]
+        out = place(where, pieces, rows * N_SHARD, out)
+    return out
 
 
 def local(

time: 106 us -> 98.9 us (0.933)
  local copies, waits for them, and re-layouts: 11.9 us -> 7.07 us
  Pallas kernels: 15.3 us -> 10.8 us
  starting transfers between devices: 48.5 us -> 50.1 us
  waiting for transfers between devices: 25.2 us -> 26.8 us
  other arithmetic: 3.55 us -> 2.48 us
    unnamed x38 -> x10, local copies, waits for them, and re-layouts: 5.14 us -> 0.89 us
    pallas_call x1, Pallas kernels: 6.93 us -> 4.04 us  [owner_update(): pl.pallas_call(state_kernel, grid=(steps,), in_specs=[pl.BlockSpec((N_REP...]
    ppermute x23, starting transfers between devices: 32.4 us -> 34.2 us  [shift(): lax.ppermute(array, axis, [(i, (i + step) % size) for i in range(size)])]
    ppermute x23, waiting for transfers between devices: 24.6 us -> 26.2 us  [shift(): lax.ppermute(array, axis, [(i, (i + step) % size) for i in range(size)])]
    pallas_call x1, Pallas kernels: 2.11 us -> 0.77 us  [arrange(): pl.pallas_call(arrange_kernel, in_specs=[pl.BlockSpec(memory_space=pltpu....]
    pallas_call x1 -> x2, Pallas kernels: 4.23 us -> 4.37 us  [place(): pl.pallas_call(functools.partial(place_kernel, count), in_specs=[pl.Block...]
  transfers between devices with their start and end apart: 25 -> 25, of which waited for: 7 -> 10; matrix products, arithmetic and copies ran while one was open for 6% -> 5% of each run, Pallas kernels for 10% -> 9%
where the time goes in v3:
time: 98.9 us; the launch traced here: 98.2 us
  starting transfers between devices  50.1 us (51%)
  waiting for transfers between devices  26.8 us (27%)
  Pallas kernels  10.8 us (11%)
  local copies, waits for them, and re-layouts  7.07 us (7%)
  other arithmetic  2.48 us (3%)
    ppermute x23, starting transfers between devices, shift(): lax.ppermute(array, axis, [(i, (i + step) % size) for i in range(size)])  34.2 us
    ppermute x23, waiting for transfers between devices, shift(): lax.ppermute(array, axis, [(i, (i + step) % size) for i in range(size)])  26.2 us
    all_to_all x1, starting transfers between devices, local(): lax.all_to_all(packed, ALL, split_axis=0, concat_axis=0, tiled=True)  11.5 us
    pallas_call x2, Pallas kernels, place(): pl.pallas_call(functools.partial(place_kernel, count), in_specs=[pl.Block...  4.37 us
    all_to_all x1, starting transfers between devices, local(): tiles = lax.all_to_all(tiles, REP, split_axis=0, concat_axis=0, tiled=True)  4.34 us
    pallas_call x1, Pallas kernels, owner_update(): pl.pallas_call(state_kernel, grid=(steps,), in_specs=[pl.BlockSpec((N_REP...  4.04 us
    transpose x1, local copies, waits for them, and re-layouts, local(): packed.transpose(4, 2, 0, 1, 3, 5)  3.51 us
  transfers between devices with their start and end apart: 25, of which 10 were waited for; matrix products, arithmetic and copies ran while one was open for 5% of the time, Pallas kernels for 9%

profile of v3, /device:TPU:1, one launch (start us, length us, event | category | flops | bytes accessed | tf_op | source)
XLA Modules:
  0.0 98.2 jit_solution(15531351484445423157)
XLA Ops:
  0.6 3.5 %copy.26 = bf16[8,2,8,8,8,128]{5,4,3,2,1,0:T(8,128)(2,1)} copy(bf16[8,2,8,8,8,128]{5,4,0,1,3,2:T(8,128)(2,1)} %bitcast.99) | data formatting | bytes 4194304 | tf_op jit(solution)/shard_map/transpose | solution.py:232
  4.2 11.5 %all-to-all-start = ((bf16[128,8,8,128]{3,2,1,0:T(8,128)(2,1)}), bf16[128,8,8,128]{3,2,1,0:T(8,128)(2,1)S(1)}, u32[]{:S(2)}, u32[]{:S(2)}) async-start(bf16[128,8,8,128]{3,2,1,0:T(8,128)(2,1)} %bitcast.97), calls=%async_computation | async-start | bytes 4194304 | tf_op jit(solution)/shard_map/all_to_all | solution.py:233
  23.9 2.0 %collective-permute-start.2 = (f32[8,3,8,128]{3,2,0,1:T(8,128)S(1)}, f32[8,3,8,128]{3,2,0,1:T(8,128)S(1)}, u32[]{:S(2)}, u32[]{:S(2)}) collective-permute-start(f32[8,3,8,128]{3,2,0,1:T(8,128)S(1)} %bitcast.109), channel_id=1, source_target_pairs={{0,6},{2,0},{4,2},{6,4},{1,7},{3,1},{5,3},{7,5},{8,14},{10,8},{12,... | collective-permute-start | bytes 294920 | tf_op jit(solution)/shard_map/ppermute | solution.py:170
  27.3 15.7 %collective-permute-done.1 = f32[8,3,8,128]{3,2,0,1:T(8,128)S(1)} collective-permute-done((f32[8,3,8,128]{3,2,0,1:T(8,128)S(1)}, f32[8,3,8,128]{3,2,0,1:T(8,128)S(1)}, u32[]{:S(2)}, u32[]{:S(2)}) %collective-permute-start.1) | collective-permute-done | bytes 98336 | tf_op jit(solution)/shard_map/ppermute | solution.py:170
  43.0 2.4 %collective-permute-done.3 = f32[8,3,8,128]{3,2,0,1:T(8,128)S(1)} collective-permute-done((f32[8,3,8,128]{3,2,0,1:T(8,128)S(1)}, f32[8,3,8,128]{3,2,0,1:T(8,128)S(1)}, u32[]{:S(2)}, u32[]{:S(2)}) %collective-permute-start.3) | collective-permute-done | bytes 98336 | tf_op jit(solution)/shard_map/ppermute | solution.py:170
  46.4 2.6 %collective-permute-start.4 = (f32[8,8,128]{2,1,0:T(8,128)S(1)}, f32[8,8,128]{2,1,0:T(8,128)S(1)}, u32[]{:S(2)}, u32[]{:S(2)}) collective-permute-start(f32[8,8,128]{2,1,0:T(8,128)S(1)} %fusion.15), channel_id=1, source_target_pairs={{0,96},{32,0},{64,32},{96,64},{1,97},{33,1},{65,33},{97,65},{2,98}... | collective-permute-start | bytes 98312 | tf_op jit(solution)/shard_map/ppermute | solution.py:170
  49.9 1.8 %collective-permute-start.19 = (f32[8,8,128]{2,1,0:T(8,128)S(1)}, f32[8,8,128]{2,1,0:T(8,128)S(1)}, u32[]{:S(2)}, u32[]{:S(2)}) collective-permute-start(f32[8,8,128]{2,1,0:T(8,128)S(1)} %convert_reduce_fusion), channel_id=1, source_target_pairs={{0,1},{1,0},{2,3},{3,2},{4,5},{5,4},{6,7},{7,6},{8,9},{9,8},{10,11... | collective-permute-start | bytes 98312 | tf_op jit(solution)/shard_map/ppermute | solution.py:170
  51.7 1.7 %collective-permute-done.5 = f32[8,8,128]{2,1,0:T(8,128)S(1)} collective-permute-done((f32[8,8,128]{2,1,0:T(8,128)S(1)}, f32[8,8,128]{2,1,0:T(8,128)S(1)}, u32[]{:S(2)}, u32[]{:S(2)}) %collective-permute-start.5) | collective-permute-done | bytes 32800 | tf_op jit(solution)/shard_map/ppermute | solution.py:170
  53.4 2.7 %collective-permute-start.7 = (f32[4,8,8,128]{3,2,1,0:T(8,128)S(1)}, f32[4,8,8,128]{3,2,1,0:T(8,128)S(1)}, u32[]{:S(2)}, u32[]{:S(2)}) collective-permute-start(f32[4,8,8,128]{3,2,1,0:T(8,128)S(1)} %pad_maximum_fusion.1.refs_0_), channel_id=1, source_target_pairs={{0,24},{8,0},{16,8},{24,16},{1,25},{9,1},{17,9},{25,17},{2,26},{10... | collective-permute-start | bytes 393224 | tf_op jit(solution)/shard_map/ppermute | solution.py:170
  58.2 1.2 %collective-permute-start.21 = (f32[2,8,8,128]{3,2,1,0:T(8,128)S(1)}, f32[2,8,8,128]{3,2,1,0:T(8,128)S(1)}, u32[]{:S(2)}, u32[]{:S(2)}) collective-permute-start(f32[2,8,8,128]{3,2,1,0:T(8,128)S(1)} %pad_maximum_fusion.2.refs_0_), channel_id=1, source_target_pairs={{0,4},{2,6},{4,0},{6,2},{1,5},{3,7},{5,1},{7,3},{8,12},{10,14},{12... | collective-permute-start | bytes 196616 | tf_op jit(solution)/shard_map/ppermute | solution.py:170
  59.4 2.1 %collective-permute-done.8.refs_2_ = f32[4,8,8,128]{3,2,1,0:T(8,128)S(1)} collective-permute-done((f32[4,8,8,128]{3,2,1,0:T(8,128)S(1)}, f32[4,8,8,128]{3,2,1,0:T(8,128)S(1)}, u32[]{:S(2)}, u32[]{:S(2)}) %collective-permute-start.8) | collective-permute-done | bytes 131104 | tf_op jit(solution)/shard_map/ppermute | solution.py:170
  61.5 1.3 %collective-permute-done.9.refs_3_ = f32[4,8,8,128]{3,2,1,0:T(8,128)S(1)} collective-permute-done((f32[4,8,8,128]{3,2,1,0:T(8,128)S(1)}, f32[4,8,8,128]{3,2,1,0:T(8,128)S(1)}, u32[]{:S(2)}, u32[]{:S(2)}) %collective-permute-start.9) | collective-permute-done | bytes 131104 | tf_op jit(solution)/shard_map/ppermute | solution.py:170
  63.9 2.4 %collective-permute-start.13 = (f32[128,1024]{1,0:T(8,128)S(1)}, f32[128,1024]{1,0:T(8,128)S(1)}, u32[]{:S(2)}, u32[]{:S(2)}) collective-permute-start(f32[128,1024]{1,0:T(8,128)S(1)} %arrange.1.refs_0_), channel_id=1, source_target_pairs={{0,6},{2,0},{4,2},{6,4},{1,7},{3,1},{5,3},{7,5},{8,14},{10,8},{12,... | collective-permute-start | bytes 1572872 | tf_op jit(solution)/shard_map/ppermute | solution.py:170
  66.4 1.6 %pick.1 = f32[16,16,8,128]{3,2,1,0:T(8,128)} custom-call(s32[16]{0:T(128)S(1)} %fusion.22.index, f32[2,8,8,128]{3,2,1,0:T(8,128)S(1)} %pad_maximum_fusion.2.refs_0_, f32[2,8,8,128]{3,2,1,0:T(8,128)S(1)} %collective-permute-done.20.refs_1_, f32[2,8,8,128]{3,2,1,0:T(8,128)S(1)} %collective-permute-done.21.refs_2_, ...), custom_call_target="tpu_custom_call" | custom-call | bytes 1048576 | tf_op jit(solution)/shard_map/pick/pallas_call | solution.py:153
  68.0 4.3 %all-to-all-start.1 = ((f32[16,16,8,128]{3,2,1,0:T(8,128)}), f32[16,16,8,128]{3,2,1,0:T(8,128)}, u32[]{:S(2)}, u32[]{:S(2)}) async-start(f32[16,16,8,128]{3,2,1,0:T(8,128)} %pick.1), calls=%async_computation.1 | async-start | bytes 2097152 | tf_op jit(solution)/shard_map/all_to_all | solution.py:269
  72.4 4.9 %collective-permute-start.16 = (f32[128,1024]{1,0:T(8,128)S(1)}, f32[128,1024]{1,0:T(8,128)S(1)}, u32[]{:S(2)}, u32[]{:S(2)}) collective-permute-start(f32[128,1024]{1,0:T(8,128)S(1)} %arrange.1.refs_0_), channel_id=1, source_target_pairs={{0,1},{1,0},{2,3},{3,2},{4,5},{5,4},{6,7},{7,6},{8,9},{9,8},{10,11... | collective-permute-start | bytes 1572872 | tf_op jit(solution)/shard_map/ppermute | solution.py:170
  77.4 2.7 %collective-permute-start.17 = (f32[128,1024]{1,0:T(8,128)S(1)}, f32[128,1024]{1,0:T(8,128)S(1)}, u32[]{:S(2)}, u32[]{:S(2)}) collective-permute-start(f32[128,1024]{1,0:T(8,128)S(1)} %collective-permute-done.10.refs_2_), channel_id=1, source_target_pairs={{0,1},{1,0},{2,3},{3,2},{4,5},{5,4},{6,7},{7,6},{8,9},{9,8},{10,11... | collective-permute-start | bytes 1572872 | tf_op jit(solution)/shard_map/ppermute | solution.py:170
  80.2 2.8 %collective-permute-start.14 = (f32[64,1024]{1,0:T(8,128)S(1)}, f32[64,1024]{1,0:T(8,128)}, u32[]{:S(2)}, u32[]{:S(2)}) collective-permute-start(f32[64,1024]{1,0:T(8,128)S(1)} %slice.26), channel_id=1, source_target_pairs={{0,6},{2,0},{4,2},{6,4},{1,7},{3,1},{5,3},{7,5},{8,14},{10,8},{12,... | collective-permute-start | bytes 786440 | tf_op jit(solution)/shard_map/ppermute | solution.py:170
  83.0 1.2 %collective-permute-done.11.refs_0_ = f32[64,1024]{1,0:T(8,128)S(1)} collective-permute-done((f32[64,1024]{1,0:T(8,128)S(1)}, f32[64,1024]{1,0:T(8,128)S(1)}, u32[]{:S(2)}, u32[]{:S(2)}) %collective-permute-start.11) | collective-permute-done | bytes 262176 | tf_op jit(solution)/shard_map/ppermute | solution.py:170
  84.2 3.3 %collective-permute-start.12 = (f32[64,1024]{1,0:T(8,128)S(1)}, f32[64,1024]{1,0:T(8,128)}, u32[]{:S(2)}, u32[]{:S(2)}) collective-permute-start(f32[64,1024]{1,0:T(8,128)S(1)} %collective-permute-done.11.refs_0_), channel_id=1, source_target_pairs={{0,1},{1,0},{2,3},{3,2},{4,5},{5,4},{6,7},{7,6},{8,9},{9,8},{10,11... | collective-permute-start | bytes 786440 | tf_op jit(solution)/shard_map/ppermute | solution.py:170
  88.2 1.4 %collective-permute-start.15 = (f32[64,1024]{1,0:T(8,128)}, f32[64,1024]{1,0:T(8,128)}, u32[]{:S(2)}, u32[]{:S(2)}) collective-permute-start(f32[64,1024]{1,0:T(8,128)} %collective-permute-done.14.refs_2_), channel_id=1, source_target_pairs={{0,1},{1,0},{2,3},{3,2},{4,5},{5,4},{6,7},{7,6},{8,9},{9,8},{10,11... | collective-permute-start | bytes 786440 | tf_op jit(solution)/shard_map/ppermute | solution.py:170
  89.7 4.0 %owner_update.1 = (f32[256,1024]{1,0:T(8,128)}, f32[256,1024]{1,0:T(8,128)}, f32[256,1024]{1,0:T(8,128)}, f32[256,1024]{1,0:T(8,128)}) custom-call(f32[16,16,8,128]{3,2,1,0:T(8,128)} %all-to-all-done.1.tiles, f32[256,1024]{1,0:T(8,128)} %bitcast.105, f32[256,1024]{1,0:T(8,128)} %bitcast.103, f32[256,1024]{1,0:T(8,128)} %bitcast.101, f32[256,1024]{1,0:T(8,128)} %bitcast.106), custom_call_target="tpu_custom_call" | custom-call | flops 5242880 | bytes 9437184 | tf_op jit(solution)/shard_map/owner_update/pallas_call | solution.py:59
  93.8 2.3 %place.2.refs_4_ = f32[1024,1024]{1,0:T(8,128)} custom-call(s32[6]{0:T(128)S(1)} %stack.87.where, f32[128,1024]{1,0:T(8,128)S(1)} %arrange.1.refs_0_, f32[128,1024]{1,0:T(8,128)S(1)} %collective-permute-done.16.refs_1_, f32[128,1024]{1,0:T(8,128)S(1)} %collective-permute-done.10.refs_2_, f32[128,1024]{1,0:T(8,128)S(1)} %collective-permute-done.17.refs_3_, ...), custom_call_target="tpu_custom_call" | custom-call | bytes 6291456 | tf_op jit(solution)/shard_map/place/pallas_call | solution.py:89
  96.1 2.1 %place.3 = f32[1024,1024]{1,0:T(8,128)} custom-call(s32[4]{0:T(128)S(1)} %pad_add_fusion.where, f32[64,1024]{1,0:T(8,128)S(1)} %collective-permute-done.11.refs_0_, f32[64,1024]{1,0:T(8,128)} %collective-permute-done.12.refs_1_, f32[64,1024]{1,0:T(8,128)} %collective-permute-done.14.refs_2_, ...), custom_call_target="tpu_custom_call", output_to_operand_aliasing={{}: (5, {})} | custom-call | bytes 2097152 | tf_op jit(solution)/shard_map/place/pallas_call | solution.py:89
  (77 shorter events, 15.7 us)
Async XLA Ops:
  4.2 41.8 %all-to-all-start = ((bf16[128,8,8,128]{3,2,1,0:T(8,128)(2,1)}), bf16[128,8,8,128]{3,2,1,0:T(8,128)(2,1)S(1)}, u32[]{:S(2)}, u32[]{:S(2)}) async-start(bf16[128,8,8,128]{3,2,1,0:T(8,128)(2,1)} %bitcast.97), calls=%async_computation | async-start | bytes 4194304 | tf_op jit(solution)/shard_map/all_to_all | solution.py:233
  23.2 19.8 %collective-permute-start.1 = (f32[8,3,8,128]{3,2,0,1:T(8,128)S(1)}, f32[8,3,8,128]{3,2,0,1:T(8,128)S(1)}, u32[]{:S(2)}, u32[]{:S(2)}) collective-permute-start(f32[8,3,8,128]{3,2,0,1:T(8,128)S(1)} %bitcast.108), channel_id=1, source_target_pairs={{0,2},{2,4},{4,6},{6,0},{1,3},{3,5},{5,7},{7,1},{8,10},{10,12},{12... | collective-permute-start | bytes 294920 | tf_op jit(solution)/shard_map/ppermute | solution.py:170
  23.9 19.0 %collective-permute-start.2 = (f32[8,3,8,128]{3,2,0,1:T(8,128)S(1)}, f32[8,3,8,128]{3,2,0,1:T(8,128)S(1)}, u32[]{:S(2)}, u32[]{:S(2)}) collective-permute-start(f32[8,3,8,128]{3,2,0,1:T(8,128)S(1)} %bitcast.109), channel_id=1, source_target_pairs={{0,6},{2,0},{4,2},{6,4},{1,7},{3,1},{5,3},{7,5},{8,14},{10,8},{12,... | collective-permute-start | bytes 294920 | tf_op jit(solution)/shard_map/ppermute | solution.py:170
  26.0 19.3 %collective-permute-start.3 = (f32[8,3,8,128]{3,2,0,1:T(8,128)S(1)}, f32[8,3,8,128]{3,2,0,1:T(8,128)S(1)}, u32[]{:S(2)}, u32[]{:S(2)}) collective-permute-start(f32[8,3,8,128]{3,2,0,1:T(8,128)S(1)} %bitcast.110), channel_id=1, source_target_pairs={{0,4},{2,6},{4,0},{6,2},{1,5},{3,7},{5,1},{7,3},{8,12},{10,14},{12... | collective-permute-start | bytes 294920 | tf_op jit(solution)/shard_map/ppermute | solution.py:170
  46.4 5.3 %collective-permute-start.4 = (f32[8,8,128]{2,1,0:T(8,128)S(1)}, f32[8,8,128]{2,1,0:T(8,128)S(1)}, u32[]{:S(2)}, u32[]{:S(2)}) collective-permute-start(f32[8,8,128]{2,1,0:T(8,128)S(1)} %fusion.15), channel_id=1, source_target_pairs={{0,96},{32,0},{64,32},{96,64},{1,97},{33,1},{65,33},{97,65},{2,98}... | collective-permute-start | bytes 98312 | tf_op jit(solution)/shard_map/ppermute | solution.py:170
  48.9 4.4 %collective-permute-start.5 = (f32[8,8,128]{2,1,0:T(8,128)S(1)}, f32[8,8,128]{2,1,0:T(8,128)S(1)}, u32[]{:S(2)}, u32[]{:S(2)}) collective-permute-start(f32[8,8,128]{2,1,0:T(8,128)S(1)} %fusion.15), channel_id=1, source_target_pairs={{0,64},{32,96},{64,0},{96,32},{1,65},{33,97},{65,1},{97,33},{2,66}... | collective-permute-start | bytes 98312 | tf_op jit(solution)/shard_map/ppermute | solution.py:170
  49.1 4.3 %collective-permute-start.6 = (f32[8,8,128]{2,1,0:T(8,128)S(1)}, f32[8,8,128]{2,1,0:T(8,128)S(1)}, u32[]{:S(2)}, u32[]{:S(2)}) collective-permute-start(f32[8,8,128]{2,1,0:T(8,128)S(1)} %fusion.15), channel_id=1, source_target_pairs={{0,32},{32,64},{64,96},{96,0},{1,33},{33,65},{65,97},{97,1},{2,34}... | collective-permute-start | bytes 98312 | tf_op jit(solution)/shard_map/ppermute | solution.py:170
  49.9 7.4 %collective-permute-start.19 = (f32[8,8,128]{2,1,0:T(8,128)S(1)}, f32[8,8,128]{2,1,0:T(8,128)S(1)}, u32[]{:S(2)}, u32[]{:S(2)}) collective-permute-start(f32[8,8,128]{2,1,0:T(8,128)S(1)} %convert_reduce_fusion), channel_id=1, source_target_pairs={{0,1},{1,0},{2,3},{3,2},{4,5},{5,4},{6,7},{7,6},{8,9},{9,8},{10,11... | collective-permute-start | bytes 98312 | tf_op jit(solution)/shard_map/ppermute | solution.py:170
  53.4 6.0 %collective-permute-start.7 = (f32[4,8,8,128]{3,2,1,0:T(8,128)S(1)}, f32[4,8,8,128]{3,2,1,0:T(8,128)S(1)}, u32[]{:S(2)}, u32[]{:S(2)}) collective-permute-start(f32[4,8,8,128]{3,2,1,0:T(8,128)S(1)} %pad_maximum_fusion.1.refs_0_), channel_id=1, source_target_pairs={{0,24},{8,0},{16,8},{24,16},{1,25},{9,1},{17,9},{25,17},{2,26},{10... | collective-permute-start | bytes 393224 | tf_op jit(solution)/shard_map/ppermute | solution.py:170
  56.1 5.4 %collective-permute-start.8 = (f32[4,8,8,128]{3,2,1,0:T(8,128)S(1)}, f32[4,8,8,128]{3,2,1,0:T(8,128)S(1)}, u32[]{:S(2)}, u32[]{:S(2)}) collective-permute-start(f32[4,8,8,128]{3,2,1,0:T(8,128)S(1)} %pad_maximum_fusion.1.refs_0_), channel_id=1, source_target_pairs={{0,16},{8,24},{16,0},{24,8},{1,17},{9,25},{17,1},{25,9},{2,18},{10... | collective-permute-start | bytes 393224 | tf_op jit(solution)/shard_map/ppermute | solution.py:170
  56.5 6.3 %collective-permute-start.9 = (f32[4,8,8,128]{3,2,1,0:T(8,128)S(1)}, f32[4,8,8,128]{3,2,1,0:T(8,128)S(1)}, u32[]{:S(2)}, u32[]{:S(2)}) collective-permute-start(f32[4,8,8,128]{3,2,1,0:T(8,128)S(1)} %pad_maximum_fusion.1.refs_0_), channel_id=1, source_target_pairs={{0,8},{8,16},{16,24},{24,0},{1,9},{9,17},{17,25},{25,1},{2,10},{10... | collective-permute-start | bytes 393224 | tf_op jit(solution)/shard_map/ppermute | solution.py:170
  57.2 9.1 %collective-permute-start.20 = (f32[2,8,8,128]{3,2,1,0:T(8,128)S(1)}, f32[2,8,8,128]{3,2,1,0:T(8,128)S(1)}, u32[]{:S(2)}, u32[]{:S(2)}) collective-permute-start(f32[2,8,8,128]{3,2,1,0:T(8,128)S(1)} %pad_maximum_fusion.2.refs_0_), channel_id=1, source_target_pairs={{0,6},{2,0},{4,2},{6,4},{1,7},{3,1},{5,3},{7,5},{8,14},{10,8},{12,... | collective-permute-start | bytes 196616 | tf_op jit(solution)/shard_map/ppermute | solution.py:170
  58.2 8.2 %collective-permute-start.21 = (f32[2,8,8,128]{3,2,1,0:T(8,128)S(1)}, f32[2,8,8,128]{3,2,1,0:T(8,128)S(1)}, u32[]{:S(2)}, u32[]{:S(2)}) collective-permute-start(f32[2,8,8,128]{3,2,1,0:T(8,128)S(1)} %pad_maximum_fusion.2.refs_0_), channel_id=1, source_target_pairs={{0,4},{2,6},{4,0},{6,2},{1,5},{3,7},{5,1},{7,3},{8,12},{10,14},{12... | collective-permute-start | bytes 196616 | tf_op jit(solution)/shard_map/ppermute | solution.py:170
  59.4 7.0 %collective-permute-start.22 = (f32[2,8,8,128]{3,2,1,0:T(8,128)S(1)}, f32[2,8,8,128]{3,2,1,0:T(8,128)S(1)}, u32[]{:S(2)}, u32[]{:S(2)}) collective-permute-start(f32[2,8,8,128]{3,2,1,0:T(8,128)S(1)} %pad_maximum_fusion.2.refs_0_), channel_id=1, source_target_pairs={{0,2},{2,4},{4,6},{6,0},{1,3},{3,5},{5,7},{7,1},{8,10},{10,12},{12... | collective-permute-start | bytes 196616 | tf_op jit(solution)/shard_map/ppermute | solution.py:170
  63.6 13.7 %collective-permute-start.10 = (f32[128,1024]{1,0:T(8,128)S(1)}, f32[128,1024]{1,0:T(8,128)S(1)}, u32[]{:S(2)}, u32[]{:S(2)}) collective-permute-start(f32[128,1024]{1,0:T(8,128)S(1)} %arrange.1.refs_0_), channel_id=1, source_target_pairs={{0,2},{2,4},{4,6},{6,0},{1,3},{3,5},{5,7},{7,1},{8,10},{10,12},{12... | collective-permute-start | bytes 1572872 | tf_op jit(solution)/shard_map/ppermute | solution.py:170
  63.9 16.1 %collective-permute-start.13 = (f32[128,1024]{1,0:T(8,128)S(1)}, f32[128,1024]{1,0:T(8,128)S(1)}, u32[]{:S(2)}, u32[]{:S(2)}) collective-permute-start(f32[128,1024]{1,0:T(8,128)S(1)} %arrange.1.refs_0_), channel_id=1, source_target_pairs={{0,6},{2,0},{4,2},{6,4},{1,7},{3,1},{5,3},{7,5},{8,14},{10,8},{12,... | collective-permute-start | bytes 1572872 | tf_op jit(solution)/shard_map/ppermute | solution.py:170
  68.0 21.7 %all-to-all-start.1 = ((f32[16,16,8,128]{3,2,1,0:T(8,128)}), f32[16,16,8,128]{3,2,1,0:T(8,128)}, u32[]{:S(2)}, u32[]{:S(2)}) async-start(f32[16,16,8,128]{3,2,1,0:T(8,128)} %pick.1), calls=%async_computation.1 | async-start | bytes 2097152 | tf_op jit(solution)/shard_map/all_to_all | solution.py:269
  72.4 21.4 %collective-permute-start.16 = (f32[128,1024]{1,0:T(8,128)S(1)}, f32[128,1024]{1,0:T(8,128)S(1)}, u32[]{:S(2)}, u32[]{:S(2)}) collective-permute-start(f32[128,1024]{1,0:T(8,128)S(1)} %arrange.1.refs_0_), channel_id=1, source_target_pairs={{0,1},{1,0},{2,3},{3,2},{4,5},{5,4},{6,7},{7,6},{8,9},{9,8},{10,11... | collective-permute-start | bytes 1572872 | tf_op jit(solution)/shard_map/ppermute | solution.py:170
  77.3 6.9 %collective-permute-start.11 = (f32[64,1024]{1,0:T(8,128)S(1)}, f32[64,1024]{1,0:T(8,128)S(1)}, u32[]{:S(2)}, u32[]{:S(2)}) collective-permute-start(f32[64,1024]{1,0:T(8,128)S(1)} %slice.25), channel_id=1, source_target_pairs={{0,2},{2,4},{4,6},{6,0},{1,3},{3,5},{5,7},{7,1},{8,10},{10,12},{12... | collective-permute-start | bytes 786440 | tf_op jit(solution)/shard_map/ppermute | solution.py:170
  77.4 16.4 %collective-permute-start.17 = (f32[128,1024]{1,0:T(8,128)S(1)}, f32[128,1024]{1,0:T(8,128)S(1)}, u32[]{:S(2)}, u32[]{:S(2)}) collective-permute-start(f32[128,1024]{1,0:T(8,128)S(1)} %collective-permute-done.10.refs_2_), channel_id=1, source_target_pairs={{0,1},{1,0},{2,3},{3,2},{4,5},{5,4},{6,7},{7,6},{8,9},{9,8},{10,11... | collective-permute-start | bytes 1572872 | tf_op jit(solution)/shard_map/ppermute | solution.py:170
  80.1 13.7 %collective-permute-start.18 = (f32[128,1024]{1,0:T(8,128)S(1)}, f32[128,1024]{1,0:T(8,128)S(1)}, u32[]{:S(2)}, u32[]{:S(2)}) collective-permute-start(f32[128,1024]{1,0:T(8,128)S(1)} %collective-permute-done.13.refs_4_), channel_id=1, source_target_pairs={{0,1},{1,0},{2,3},{3,2},{4,5},{5,4},{6,7},{7,6},{8,9},{9,8},{10,11... | collective-permute-start | bytes 1572872 | tf_op jit(solution)/shard_map/ppermute | solution.py:170
  80.2 8.0 %collective-permute-start.14 = (f32[64,1024]{1,0:T(8,128)S(1)}, f32[64,1024]{1,0:T(8,128)}, u32[]{:S(2)}, u32[]{:S(2)}) collective-permute-start(f32[64,1024]{1,0:T(8,128)S(1)} %slice.26), channel_id=1, source_target_pairs={{0,6},{2,0},{4,2},{6,4},{1,7},{3,1},{5,3},{7,5},{8,14},{10,8},{12,... | collective-permute-start | bytes 786440 | tf_op jit(solution)/shard_map/ppermute | solution.py:170
  84.2 11.8 %collective-permute-start.12 = (f32[64,1024]{1,0:T(8,128)S(1)}, f32[64,1024]{1,0:T(8,128)}, u32[]{:S(2)}, u32[]{:S(2)}) collective-permute-start(f32[64,1024]{1,0:T(8,128)S(1)} %collective-permute-done.11.refs_0_), channel_id=1, source_target_pairs={{0,1},{1,0},{2,3},{3,2},{4,5},{5,4},{6,7},{7,6},{8,9},{9,8},{10,11... | collective-permute-start | bytes 786440 | tf_op jit(solution)/shard_map/ppermute | solution.py:170
  88.2 7.9 %collective-permute-start.15 = (f32[64,1024]{1,0:T(8,128)}, f32[64,1024]{1,0:T(8,128)}, u32[]{:S(2)}, u32[]{:S(2)}) collective-permute-start(f32[64,1024]{1,0:T(8,128)} %collective-permute-done.14.refs_2_), channel_id=1, source_target_pairs={{0,1},{1,0},{2,3},{3,2},{4,5},{5,4},{6,7},{7,6},{8,9},{9,8},{10,11... | collective-permute-start | bytes 786440 | tf_op jit(solution)/shard_map/ppermute | solution.py:170
  (6 other events, 49.7 us)

commit v4 on v3

--- a/solution.py
+++ b/solution.py
@@ -132,13 +132,12 @@
     )(at, *groups)
 
 
-def pick_kernel(index, *refs):
-    groups, out, window = refs[:4], refs[4], refs[5]
-    units = groups[0].shape[1]
-    for far in range(4):
-        for core in range(2):
-            for unit in range(units):
-                window[(far * 2 + core) * units + unit] = groups[far][core, unit]
+def pick_kernel(index, same, other, out, window):
+    near, units = same.shape[:2]
+    for step in range(near):
+        for unit in range(units):
+            window[step * units + unit] = same[step, unit]
+            window[(near + step) * units + unit] = other[step, unit]
     for slot in range(out.shape[1]):
         at = index[slot]
         tile = window[jnp.maximum(at, 0)]
@@ -147,22 +146,57 @@
             out[copy, slot] = tile
 
 
-def pick(index, groups):
-    units = groups[0].shape[1]
-    slots = index.shape[0]
+def pick(index, same, other):
+    slots, units = index.shape[0], same.shape[0] * same.shape[1]
     return pl.pallas_call(
         pick_kernel,
         in_specs=[pl.BlockSpec(memory_space=pltpu.SMEM)]
-        + [pl.BlockSpec(memory_space=pltpu.VMEM)] * 4,
+        + [pl.BlockSpec(memory_space=pltpu.VMEM)] * 2,
         out_specs=pl.BlockSpec(memory_space=pltpu.VMEM),
         out_shape=jax.ShapeDtypeStruct((N_REP, slots, SUB, LANES), jnp.float32),
-        scratch_shapes=[pltpu.VMEM((8 * units, SUB, LANES), jnp.float32)],
+        scratch_shapes=[pltpu.VMEM((2 * units, SUB, LANES), jnp.float32)],
         compiler_params=pltpu.CompilerParams(vmem_limit_bytes=4 << 20),
         cost_estimate=pl.CostEstimate(
             flops=0, bytes_accessed=4 * N_REP * slots * SUB * LANES, transcendentals=0
         ),
         name="pick",
-    )(index, *groups)
+    )(index, same, other)
+
+
+def tile_kernel(given, out, held, sems):
+    steps = held.shape[0]
+    units = held.shape[1]
+    loads = [
+        pltpu.make_async_copy(given.at[pl.ds(step * units, units)], held.at[step], sems.at[step])
+        for step in range(steps)
+    ]
+    for load in loads:
+        load.start()
+    for step in range(steps):
+        loads[step].wait()
+        for block in range(out.shape[0] // 2):
+            lanes = pl.ds(block * LANES, LANES)
+            for half in range(2):
+                out[block * 2 + half, pl.ds(step * units, units)] = held[step, :, half, :, lanes]
+
+
+def tile_order(gradient):
+    rows, width = gradient.shape
+    units = rows // UNIT
+    return pl.pallas_call(
+        tile_kernel,
+        in_specs=[pl.BlockSpec(memory_space=pl.ANY)],
+        out_specs=pl.BlockSpec(memory_space=pltpu.VMEM),
+        out_shape=jax.ShapeDtypeStruct((N_REP, units, SUB, LANES), gradient.dtype),
+        scratch_shapes=[
+            pltpu.VMEM((8, units // 8, 2, SUB, width), gradient.dtype),
+            pltpu.SemaphoreType.DMA((8,)),
+        ],
+        cost_estimate=pl.CostEstimate(
+            flops=0, bytes_accessed=4 * rows * width, transcendentals=0
+        ),
+        name="tile_order",
+    )(gradient.reshape(units, 2, SUB, width))
 
 
 def shift(array, axis, step):
@@ -228,8 +262,7 @@
     slot_unit = jnp.sum(jnp.where(held, source[None, :] + slot_first[:, None], 0), axis=1) // UNIT
     slot_used = jnp.any(held, axis=1)
 
-    packed = gradient.reshape(N_SHARD, own_units, 2, SUB, blocks, LANES)
-    packed = packed.transpose(4, 2, 0, 1, 3, 5).reshape(N_REP * N_SHARD, own_units, SUB, LANES)
+    packed = tile_order(gradient).reshape(N_REP * N_SHARD, own_units, SUB, LANES)
     received = lax.all_to_all(packed, ALL, split_axis=0, concat_axis=0, tiled=True)
     summed = jnp.sum(received, axis=0, dtype=jnp.float32)
 
@@ -260,12 +293,12 @@
     lines = arrange(jnp.stack([z, y]).astype(jnp.int32), far)
     new_params = gather_lines(lines)
 
-    pair = jnp.stack([summed, shift(summed, "core", 1)])
-    window = [pair] + [shift(pair, "x", step) for step in (3, 2, 1)]
+    same = jnp.stack([summed] + [shift(summed, "x", step) for step in (3, 2, 1)])
+    other = shift(same, "core", 1)
     from_shard = slot_unit // own_units
-    place_of = (from_shard // 2 - x + 4) % 4 * 2 + (from_shard + core) % 2
-    index = place_of * own_units + slot_unit % own_units
-    tiles = pick(jnp.where(slot_used, index, -1).astype(jnp.int32), window)
+    index = (from_shard + core) % 2 * 4 + (from_shard // 2 - x + 4) % 4
+    index = index * own_units + slot_unit % own_units
+    tiles = pick(jnp.where(slot_used, index, -1).astype(jnp.int32), same, other)
     tiles = lax.all_to_all(tiles, REP, split_axis=0, concat_axis=0, tiled=True)
     outs = owner_update(tiles, master[0], moment_one[0], moment_two[0], average[0])
     return (new_params, *(o[None] for o in outs))

time: 98.9 us -> 98.1 us (level)
  local copies, waits for them, and re-layouts: 7.07 us -> 3.57 us
  Pallas kernels: 10.8 us -> 13.7 us
  waiting for transfers between devices: 26.8 us -> 25.4 us
    transpose x1 -> x0, local copies, waits for them, and re-layouts: 3.51 us -> none  [local(): packed.transpose(4, 2, 0, 1, 3, 5)]
    pallas_call x0 -> x1, Pallas kernels: none -> 2.94 us  [tile_order(): pl.pallas_call(tile_kernel, in_specs=[pl.BlockSpec(memory_space=pl.ANY)],...]
    ppermute x23, waiting for transfers between devices: 26.2 us -> 24.8 us  [shift(): lax.ppermute(array, axis, [(i, (i + step) % size) for i in range(size)])]
where the time goes in v4:
time: 98.1 us; the launch traced here: 96.9 us
  starting transfers between devices  50.8 us (52%)
  waiting for transfers between devices  25.4 us (26%)
  Pallas kernels  13.7 us (14%)
  local copies, waits for them, and re-layouts  3.57 us (4%)
  other arithmetic  2.48 us (3%)
    ppermute x23, starting transfers between devices, shift(): lax.ppermute(array, axis, [(i, (i + step) % size) for i in range(size)])  34.9 us
    ppermute x23, waiting for transfers between devices, shift(): lax.ppermute(array, axis, [(i, (i + step) % size) for i in range(size)])  24.8 us
    all_to_all x1, starting transfers between devices, local(): lax.all_to_all(packed, ALL, split_axis=0, concat_axis=0, tiled=True)  11.5 us
    pallas_call x2, Pallas kernels, place(): pl.pallas_call(functools.partial(place_kernel, count), in_specs=[pl.Block...  4.37 us
    all_to_all x1, starting transfers between devices, local(): tiles = lax.all_to_all(tiles, REP, split_axis=0, concat_axis=0, tiled=True)  4.34 us
    pallas_call x1, Pallas kernels, owner_update(): pl.pallas_call(state_kernel, grid=(steps,), in_specs=[pl.BlockSpec((N_REP...  4.04 us
    pallas_call x1, Pallas kernels, tile_order(): pl.pallas_call(tile_kernel, in_specs=[pl.BlockSpec(memory_space=pl.ANY)],...  2.94 us
  transfers between devices with their start and end apart: 25, of which 10 were waited for; matrix products, arithmetic and copies ran while one was open for 5% of the time, Pallas kernels for 9%

profile of v4, /device:TPU:1, one launch (start us, length us, event | category | flops | bytes accessed | tf_op | source)
XLA Modules:
  0.0 96.9 jit_solution(1001939276565489022)
XLA Ops:
  0.6 2.9 %tile_order.1 = bf16[16,64,8,128]{3,2,1,0:T(8,128)(2,1)} custom-call(bf16[64,2,8,1024]{3,2,1,0:T(8,128)(2,1)} %bitcast.93), custom_call_target="tpu_custom_call" | custom-call | bytes 4194304 | tf_op jit(solution)/shard_map/tile_order/pallas_call | solution.py:186
  3.6 11.5 %all-to-all-start = ((bf16[128,8,8,128]{3,2,1,0:T(8,128)(2,1)}), bf16[128,8,8,128]{3,2,1,0:T(8,128)(2,1)S(1)}, u32[]{:S(2)}, u32[]{:S(2)}) async-start(bf16[128,8,8,128]{3,2,1,0:T(8,128)(2,1)} %bitcast.91), calls=%async_computation | async-start | bytes 4194304 | tf_op jit(solution)/shard_map/all_to_all | solution.py:266
  20.4 1.2 %collective-permute-done = f32[4,8,3,8,128]{4,3,2,1,0:T(8,128)S(1)} collective-permute-done((f32[4,8,3,8,128]{4,3,2,1,0:T(8,128)S(1)}, f32[4,8,3,8,128]{4,3,2,1,0:T(8,128)S(1)}, u32[]{:S(2)}, u32[]{:S(2)}) %collective-permute-start) | collective-permute-done | bytes 393248 | tf_op jit(solution)/shard_map/ppermute | solution.py:204
  23.4 2.0 %collective-permute-start.2 = (f32[8,3,8,128]{3,2,0,1:T(8,128)S(1)}, f32[8,3,8,128]{3,2,0,1:T(8,128)S(1)}, u32[]{:S(2)}, u32[]{:S(2)}) collective-permute-start(f32[8,3,8,128]{3,2,0,1:T(8,128)S(1)} %bitcast.103), channel_id=1, source_target_pairs={{0,6},{2,0},{4,2},{6,4},{1,7},{3,1},{5,3},{7,5},{8,14},{10,8},{12,... | collective-permute-start | bytes 294920 | tf_op jit(solution)/shard_map/ppermute | solution.py:204
  26.7 15.7 %collective-permute-done.1 = f32[8,3,8,128]{3,2,0,1:T(8,128)S(1)} collective-permute-done((f32[8,3,8,128]{3,2,0,1:T(8,128)S(1)}, f32[8,3,8,128]{3,2,0,1:T(8,128)S(1)}, u32[]{:S(2)}, u32[]{:S(2)}) %collective-permute-start.1) | collective-permute-done | bytes 98336 | tf_op jit(solution)/shard_map/ppermute | solution.py:204
  42.4 2.4 %collective-permute-done.3 = f32[8,3,8,128]{3,2,0,1:T(8,128)S(1)} collective-permute-done((f32[8,3,8,128]{3,2,0,1:T(8,128)S(1)}, f32[8,3,8,128]{3,2,0,1:T(8,128)S(1)}, u32[]{:S(2)}, u32[]{:S(2)}) %collective-permute-start.3) | collective-permute-done | bytes 98336 | tf_op jit(solution)/shard_map/ppermute | solution.py:204
  45.8 2.6 %collective-permute-start.4 = (f32[8,8,128]{2,1,0:T(8,128)S(1)}, f32[8,8,128]{2,1,0:T(8,128)S(1)}, u32[]{:S(2)}, u32[]{:S(2)}) collective-permute-start(f32[8,8,128]{2,1,0:T(8,128)S(1)} %fusion.15), channel_id=1, source_target_pairs={{0,96},{32,0},{64,32},{96,64},{1,97},{33,1},{65,33},{97,65},{2,98}... | collective-permute-start | bytes 98312 | tf_op jit(solution)/shard_map/ppermute | solution.py:204
  50.3 1.2 %collective-permute-start.20 = (f32[8,8,128]{2,1,0:T(8,128)S(1)}, f32[8,8,128]{2,1,0:T(8,128)S(1)}, u32[]{:S(2)}, u32[]{:S(2)}) collective-permute-start(f32[8,8,128]{2,1,0:T(8,128)S(1)} %convert_reduce_fusion), channel_id=1, source_target_pairs={{0,4},{2,6},{4,0},{6,2},{1,5},{3,7},{5,1},{7,3},{8,12},{10,14},{12... | collective-permute-start | bytes 98312 | tf_op jit(solution)/shard_map/ppermute | solution.py:204
  51.5 1.3 %collective-permute-done.5 = f32[8,8,128]{2,1,0:T(8,128)S(1)} collective-permute-done((f32[8,8,128]{2,1,0:T(8,128)S(1)}, f32[8,8,128]{2,1,0:T(8,128)S(1)}, u32[]{:S(2)}, u32[]{:S(2)}) %collective-permute-start.5) | collective-permute-done | bytes 32800 | tf_op jit(solution)/shard_map/ppermute | solution.py:204
  52.9 2.7 %collective-permute-start.7 = (f32[4,8,8,128]{3,2,1,0:T(8,128)S(1)}, f32[4,8,8,128]{3,2,1,0:T(8,128)S(1)}, u32[]{:S(2)}, u32[]{:S(2)}) collective-permute-start(f32[4,8,8,128]{3,2,1,0:T(8,128)S(1)} %pad_maximum_fusion.1.refs_0_), channel_id=1, source_target_pairs={{0,24},{8,0},{16,8},{24,16},{1,25},{9,1},{17,9},{25,17},{2,26},{10... | collective-permute-start | bytes 393224 | tf_op jit(solution)/shard_map/ppermute | solution.py:204
  56.7 3.4 %collective-permute-start.22 = (f32[4,8,8,128]{3,2,1,0:T(8,128)S(1)}, f32[4,8,8,128]{3,2,1,0:T(8,128)S(1)}, u32[]{:S(2)}, u32[]{:S(2)}) collective-permute-start(f32[4,8,8,128]{3,2,1,0:T(8,128)S(1)} %pad_maximum_fusion.2.same), channel_id=1, source_target_pairs={{0,1},{1,0},{2,3},{3,2},{4,5},{5,4},{6,7},{7,6},{8,9},{9,8},{10,11... | collective-permute-start | bytes 393224 | tf_op jit(solution)/shard_map/ppermute | solution.py:204
  61.0 1.3 %collective-permute-done.9.refs_3_ = f32[4,8,8,128]{3,2,1,0:T(8,128)S(1)} collective-permute-done((f32[4,8,8,128]{3,2,1,0:T(8,128)S(1)}, f32[4,8,8,128]{3,2,1,0:T(8,128)S(1)}, u32[]{:S(2)}, u32[]{:S(2)}) %collective-permute-start.9) | collective-permute-done | bytes 131104 | tf_op jit(solution)/shard_map/ppermute | solution.py:204
  63.4 2.4 %collective-permute-start.13 = (f32[128,1024]{1,0:T(8,128)S(1)}, f32[128,1024]{1,0:T(8,128)S(1)}, u32[]{:S(2)}, u32[]{:S(2)}) collective-permute-start(f32[128,1024]{1,0:T(8,128)S(1)} %arrange.1.refs_0_), channel_id=1, source_target_pairs={{0,6},{2,0},{4,2},{6,4},{1,7},{3,1},{5,3},{7,5},{8,14},{10,8},{12,... | collective-permute-start | bytes 1572872 | tf_op jit(solution)/shard_map/ppermute | solution.py:204
  65.8 1.6 %pick.1 = f32[16,16,8,128]{3,2,1,0:T(8,128)} custom-call(s32[16]{0:T(128)S(1)} %fusion.22.index, f32[4,8,8,128]{3,2,1,0:T(8,128)S(1)} %pad_maximum_fusion.2.same, f32[4,8,8,128]{3,2,1,0:T(8,128)S(1)} %collective-permute-done.22.other), custom_call_target="tpu_custom_call" | custom-call | bytes 1048576 | tf_op jit(solution)/shard_map/pick/pallas_call | solution.py:151
  67.5 4.3 %all-to-all-start.1 = ((f32[16,16,8,128]{3,2,1,0:T(8,128)}), f32[16,16,8,128]{3,2,1,0:T(8,128)}, u32[]{:S(2)}, u32[]{:S(2)}) async-start(f32[16,16,8,128]{3,2,1,0:T(8,128)} %pick.1), calls=%async_computation.1 | async-start | bytes 2097152 | tf_op jit(solution)/shard_map/all_to_all | solution.py:302
  71.8 4.5 %collective-permute-start.16 = (f32[128,1024]{1,0:T(8,128)S(1)}, f32[128,1024]{1,0:T(8,128)S(1)}, u32[]{:S(2)}, u32[]{:S(2)}) collective-permute-start(f32[128,1024]{1,0:T(8,128)S(1)} %arrange.1.refs_0_), channel_id=1, source_target_pairs={{0,1},{1,0},{2,3},{3,2},{4,5},{5,4},{6,7},{7,6},{8,9},{9,8},{10,11... | collective-permute-start | bytes 1572872 | tf_op jit(solution)/shard_map/ppermute | solution.py:204
  76.5 2.4 %collective-permute-start.17 = (f32[128,1024]{1,0:T(8,128)S(1)}, f32[128,1024]{1,0:T(8,128)S(1)}, u32[]{:S(2)}, u32[]{:S(2)}) collective-permute-start(f32[128,1024]{1,0:T(8,128)S(1)} %collective-permute-done.10.refs_2_), channel_id=1, source_target_pairs={{0,1},{1,0},{2,3},{3,2},{4,5},{5,4},{6,7},{7,6},{8,9},{9,8},{10,11... | collective-permute-start | bytes 1572872 | tf_op jit(solution)/shard_map/ppermute | solution.py:204
  79.0 2.8 %collective-permute-start.14 = (f32[64,1024]{1,0:T(8,128)S(1)}, f32[64,1024]{1,0:T(8,128)}, u32[]{:S(2)}, u32[]{:S(2)}) collective-permute-start(f32[64,1024]{1,0:T(8,128)S(1)} %slice.26), channel_id=1, source_target_pairs={{0,6},{2,0},{4,2},{6,4},{1,7},{3,1},{5,3},{7,5},{8,14},{10,8},{12,... | collective-permute-start | bytes 786440 | tf_op jit(solution)/shard_map/ppermute | solution.py:204
  81.8 1.5 %collective-permute-done.11.refs_0_ = f32[64,1024]{1,0:T(8,128)S(1)} collective-permute-done((f32[64,1024]{1,0:T(8,128)S(1)}, f32[64,1024]{1,0:T(8,128)S(1)}, u32[]{:S(2)}, u32[]{:S(2)}) %collective-permute-start.11) | collective-permute-done | bytes 262176 | tf_op jit(solution)/shard_map/ppermute | solution.py:204
  83.3 3.1 %collective-permute-start.12 = (f32[64,1024]{1,0:T(8,128)S(1)}, f32[64,1024]{1,0:T(8,128)}, u32[]{:S(2)}, u32[]{:S(2)}) collective-permute-start(f32[64,1024]{1,0:T(8,128)S(1)} %collective-permute-done.11.refs_0_), channel_id=1, source_target_pairs={{0,1},{1,0},{2,3},{3,2},{4,5},{5,4},{6,7},{7,6},{8,9},{9,8},{10,11... | collective-permute-start | bytes 786440 | tf_op jit(solution)/shard_map/ppermute | solution.py:204
  87.0 1.4 %collective-permute-start.15 = (f32[64,1024]{1,0:T(8,128)}, f32[64,1024]{1,0:T(8,128)}, u32[]{:S(2)}, u32[]{:S(2)}) collective-permute-start(f32[64,1024]{1,0:T(8,128)} %collective-permute-done.14.refs_2_), channel_id=1, source_target_pairs={{0,1},{1,0},{2,3},{3,2},{4,5},{5,4},{6,7},{7,6},{8,9},{9,8},{10,11... | collective-permute-start | bytes 786440 | tf_op jit(solution)/shard_map/ppermute | solution.py:204
  88.5 4.0 %owner_update.1 = (f32[256,1024]{1,0:T(8,128)}, f32[256,1024]{1,0:T(8,128)}, f32[256,1024]{1,0:T(8,128)}, f32[256,1024]{1,0:T(8,128)}) custom-call(f32[16,16,8,128]{3,2,1,0:T(8,128)} %all-to-all-done.1.tiles, f32[256,1024]{1,0:T(8,128)} %bitcast.99, f32[256,1024]{1,0:T(8,128)} %bitcast.97, f32[256,1024]{1,0:T(8,128)} %bitcast.95, f32[256,1024]{1,0:T(8,128)} %bitcast.100), custom_call_target="tpu_custom_call" | custom-call | flops 5242880 | bytes 9437184 | tf_op jit(solution)/shard_map/owner_update/pallas_call | solution.py:59
  92.5 2.3 %place.2.refs_4_ = f32[1024,1024]{1,0:T(8,128)} custom-call(s32[6]{0:T(128)S(1)} %stack.93.where, f32[128,1024]{1,0:T(8,128)S(1)} %arrange.1.refs_0_, f32[128,1024]{1,0:T(8,128)S(1)} %collective-permute-done.16.refs_1_, f32[128,1024]{1,0:T(8,128)S(1)} %collective-permute-done.10.refs_2_, f32[128,1024]{1,0:T(8,128)S(1)} %collective-permute-done.17.refs_3_, ...), custom_call_target="tpu_custom_call" | custom-call | bytes 6291456 | tf_op jit(solution)/shard_map/place/pallas_call | solution.py:89
  94.8 2.1 %place.3 = f32[1024,1024]{1,0:T(8,128)} custom-call(s32[4]{0:T(128)S(1)} %pad_add_fusion.where, f32[64,1024]{1,0:T(8,128)S(1)} %collective-permute-done.11.refs_0_, f32[64,1024]{1,0:T(8,128)} %collective-permute-done.12.refs_1_, f32[64,1024]{1,0:T(8,128)} %collective-permute-done.14.refs_2_, ...), custom_call_target="tpu_custom_call", output_to_operand_aliasing={{}: (5, {})} | custom-call | bytes 2097152 | tf_op jit(solution)/shard_map/place/pallas_call | solution.py:89
  (77 shorter events, 15.4 us)
Async XLA Ops:
  3.6 41.8 %all-to-all-start = ((bf16[128,8,8,128]{3,2,1,0:T(8,128)(2,1)}), bf16[128,8,8,128]{3,2,1,0:T(8,128)(2,1)S(1)}, u32[]{:S(2)}, u32[]{:S(2)}) async-start(bf16[128,8,8,128]{3,2,1,0:T(8,128)(2,1)} %bitcast.91), calls=%async_computation | async-start | bytes 4194304 | tf_op jit(solution)/shard_map/all_to_all | solution.py:266
  22.6 19.8 %collective-permute-start.1 = (f32[8,3,8,128]{3,2,0,1:T(8,128)S(1)}, f32[8,3,8,128]{3,2,0,1:T(8,128)S(1)}, u32[]{:S(2)}, u32[]{:S(2)}) collective-permute-start(f32[8,3,8,128]{3,2,0,1:T(8,128)S(1)} %bitcast.102), channel_id=1, source_target_pairs={{0,2},{2,4},{4,6},{6,0},{1,3},{3,5},{5,7},{7,1},{8,10},{10,12},{12... | collective-permute-start | bytes 294920 | tf_op jit(solution)/shard_map/ppermute | solution.py:204
  23.4 19.0 %collective-permute-start.2 = (f32[8,3,8,128]{3,2,0,1:T(8,128)S(1)}, f32[8,3,8,128]{3,2,0,1:T(8,128)S(1)}, u32[]{:S(2)}, u32[]{:S(2)}) collective-permute-start(f32[8,3,8,128]{3,2,0,1:T(8,128)S(1)} %bitcast.103), channel_id=1, source_target_pairs={{0,6},{2,0},{4,2},{6,4},{1,7},{3,1},{5,3},{7,5},{8,14},{10,8},{12,... | collective-permute-start | bytes 294920 | tf_op jit(solution)/shard_map/ppermute | solution.py:204
  25.5 19.3 %collective-permute-start.3 = (f32[8,3,8,128]{3,2,0,1:T(8,128)S(1)}, f32[8,3,8,128]{3,2,0,1:T(8,128)S(1)}, u32[]{:S(2)}, u32[]{:S(2)}) collective-permute-start(f32[8,3,8,128]{3,2,0,1:T(8,128)S(1)} %bitcast.104), channel_id=1, source_target_pairs={{0,4},{2,6},{4,0},{6,2},{1,5},{3,7},{5,1},{7,3},{8,12},{10,14},{12... | collective-permute-start | bytes 294920 | tf_op jit(solution)/shard_map/ppermute | solution.py:204
  45.8 5.7 %collective-permute-start.4 = (f32[8,8,128]{2,1,0:T(8,128)S(1)}, f32[8,8,128]{2,1,0:T(8,128)S(1)}, u32[]{:S(2)}, u32[]{:S(2)}) collective-permute-start(f32[8,8,128]{2,1,0:T(8,128)S(1)} %fusion.15), channel_id=1, source_target_pairs={{0,96},{32,0},{64,32},{96,64},{1,97},{33,1},{65,33},{97,65},{2,98}... | collective-permute-start | bytes 98312 | tf_op jit(solution)/shard_map/ppermute | solution.py:204
  48.4 4.4 %collective-permute-start.5 = (f32[8,8,128]{2,1,0:T(8,128)S(1)}, f32[8,8,128]{2,1,0:T(8,128)S(1)}, u32[]{:S(2)}, u32[]{:S(2)}) collective-permute-start(f32[8,8,128]{2,1,0:T(8,128)S(1)} %fusion.15), channel_id=1, source_target_pairs={{0,64},{32,96},{64,0},{96,32},{1,65},{33,97},{65,1},{97,33},{2,66}... | collective-permute-start | bytes 98312 | tf_op jit(solution)/shard_map/ppermute | solution.py:204
  48.5 4.3 %collective-permute-start.6 = (f32[8,8,128]{2,1,0:T(8,128)S(1)}, f32[8,8,128]{2,1,0:T(8,128)S(1)}, u32[]{:S(2)}, u32[]{:S(2)}) collective-permute-start(f32[8,8,128]{2,1,0:T(8,128)S(1)} %fusion.15), channel_id=1, source_target_pairs={{0,32},{32,64},{64,96},{96,0},{1,33},{33,65},{65,97},{97,1},{2,34}... | collective-permute-start | bytes 98312 | tf_op jit(solution)/shard_map/ppermute | solution.py:204
  49.3 6.6 %collective-permute-start.19 = (f32[8,8,128]{2,1,0:T(8,128)S(1)}, f32[8,8,128]{2,1,0:T(8,128)S(1)}, u32[]{:S(2)}, u32[]{:S(2)}) collective-permute-start(f32[8,8,128]{2,1,0:T(8,128)S(1)} %convert_reduce_fusion), channel_id=1, source_target_pairs={{0,6},{2,0},{4,2},{6,4},{1,7},{3,1},{5,3},{7,5},{8,14},{10,8},{12,... | collective-permute-start | bytes 98312 | tf_op jit(solution)/shard_map/ppermute | solution.py:204
  50.3 6.4 %collective-permute-start.20 = (f32[8,8,128]{2,1,0:T(8,128)S(1)}, f32[8,8,128]{2,1,0:T(8,128)S(1)}, u32[]{:S(2)}, u32[]{:S(2)}) collective-permute-start(f32[8,8,128]{2,1,0:T(8,128)S(1)} %convert_reduce_fusion), channel_id=1, source_target_pairs={{0,4},{2,6},{4,0},{6,2},{1,5},{3,7},{5,1},{7,3},{8,12},{10,14},{12... | collective-permute-start | bytes 98312 | tf_op jit(solution)/shard_map/ppermute | solution.py:204
  51.5 5.2 %collective-permute-start.21 = (f32[8,8,128]{2,1,0:T(8,128)S(1)}, f32[8,8,128]{2,1,0:T(8,128)S(1)}, u32[]{:S(2)}, u32[]{:S(2)}) collective-permute-start(f32[8,8,128]{2,1,0:T(8,128)S(1)} %convert_reduce_fusion), channel_id=1, source_target_pairs={{0,2},{2,4},{4,6},{6,0},{1,3},{3,5},{5,7},{7,1},{8,10},{10,12},{12... | collective-permute-start | bytes 98312 | tf_op jit(solution)/shard_map/ppermute | solution.py:204
  52.9 7.3 %collective-permute-start.7 = (f32[4,8,8,128]{3,2,1,0:T(8,128)S(1)}, f32[4,8,8,128]{3,2,1,0:T(8,128)S(1)}, u32[]{:S(2)}, u32[]{:S(2)}) collective-permute-start(f32[4,8,8,128]{3,2,1,0:T(8,128)S(1)} %pad_maximum_fusion.1.refs_0_), channel_id=1, source_target_pairs={{0,24},{8,0},{16,8},{24,16},{1,25},{9,1},{17,9},{25,17},{2,26},{10... | collective-permute-start | bytes 393224 | tf_op jit(solution)/shard_map/ppermute | solution.py:204
  55.5 5.4 %collective-permute-start.8 = (f32[4,8,8,128]{3,2,1,0:T(8,128)S(1)}, f32[4,8,8,128]{3,2,1,0:T(8,128)S(1)}, u32[]{:S(2)}, u32[]{:S(2)}) collective-permute-start(f32[4,8,8,128]{3,2,1,0:T(8,128)S(1)} %pad_maximum_fusion.1.refs_0_), channel_id=1, source_target_pairs={{0,16},{8,24},{16,0},{24,8},{1,17},{9,25},{17,1},{25,9},{2,18},{10... | collective-permute-start | bytes 393224 | tf_op jit(solution)/shard_map/ppermute | solution.py:204
  56.0 6.3 %collective-permute-start.9 = (f32[4,8,8,128]{3,2,1,0:T(8,128)S(1)}, f32[4,8,8,128]{3,2,1,0:T(8,128)S(1)}, u32[]{:S(2)}, u32[]{:S(2)}) collective-permute-start(f32[4,8,8,128]{3,2,1,0:T(8,128)S(1)} %pad_maximum_fusion.1.refs_0_), channel_id=1, source_target_pairs={{0,8},{8,16},{16,24},{24,0},{1,9},{9,17},{17,25},{25,1},{2,10},{10... | collective-permute-start | bytes 393224 | tf_op jit(solution)/shard_map/ppermute | solution.py:204
  56.7 9.1 %collective-permute-start.22 = (f32[4,8,8,128]{3,2,1,0:T(8,128)S(1)}, f32[4,8,8,128]{3,2,1,0:T(8,128)S(1)}, u32[]{:S(2)}, u32[]{:S(2)}) collective-permute-start(f32[4,8,8,128]{3,2,1,0:T(8,128)S(1)} %pad_maximum_fusion.2.same), channel_id=1, source_target_pairs={{0,1},{1,0},{2,3},{3,2},{4,5},{5,4},{6,7},{7,6},{8,9},{9,8},{10,11... | collective-permute-start | bytes 393224 | tf_op jit(solution)/shard_map/ppermute | solution.py:204
  63.0 13.3 %collective-permute-start.10 = (f32[128,1024]{1,0:T(8,128)S(1)}, f32[128,1024]{1,0:T(8,128)S(1)}, u32[]{:S(2)}, u32[]{:S(2)}) collective-permute-start(f32[128,1024]{1,0:T(8,128)S(1)} %arrange.1.refs_0_), channel_id=1, source_target_pairs={{0,2},{2,4},{4,6},{6,0},{1,3},{3,5},{5,7},{7,1},{8,10},{10,12},{12... | collective-permute-start | bytes 1572872 | tf_op jit(solution)/shard_map/ppermute | solution.py:204
  63.4 15.4 %collective-permute-start.13 = (f32[128,1024]{1,0:T(8,128)S(1)}, f32[128,1024]{1,0:T(8,128)S(1)}, u32[]{:S(2)}, u32[]{:S(2)}) collective-permute-start(f32[128,1024]{1,0:T(8,128)S(1)} %arrange.1.refs_0_), channel_id=1, source_target_pairs={{0,6},{2,0},{4,2},{6,4},{1,7},{3,1},{5,3},{7,5},{8,14},{10,8},{12,... | collective-permute-start | bytes 1572872 | tf_op jit(solution)/shard_map/ppermute | solution.py:204
  67.5 21.0 %all-to-all-start.1 = ((f32[16,16,8,128]{3,2,1,0:T(8,128)}), f32[16,16,8,128]{3,2,1,0:T(8,128)}, u32[]{:S(2)}, u32[]{:S(2)}) async-start(f32[16,16,8,128]{3,2,1,0:T(8,128)} %pick.1), calls=%async_computation.1 | async-start | bytes 2097152 | tf_op jit(solution)/shard_map/all_to_all | solution.py:302
  71.8 20.7 %collective-permute-start.16 = (f32[128,1024]{1,0:T(8,128)S(1)}, f32[128,1024]{1,0:T(8,128)S(1)}, u32[]{:S(2)}, u32[]{:S(2)}) collective-permute-start(f32[128,1024]{1,0:T(8,128)S(1)} %arrange.1.refs_0_), channel_id=1, source_target_pairs={{0,1},{1,0},{2,3},{3,2},{4,5},{5,4},{6,7},{7,6},{8,9},{9,8},{10,11... | collective-permute-start | bytes 1572872 | tf_op jit(solution)/shard_map/ppermute | solution.py:204
  76.4 6.9 %collective-permute-start.11 = (f32[64,1024]{1,0:T(8,128)S(1)}, f32[64,1024]{1,0:T(8,128)S(1)}, u32[]{:S(2)}, u32[]{:S(2)}) collective-permute-start(f32[64,1024]{1,0:T(8,128)S(1)} %slice.25), channel_id=1, source_target_pairs={{0,2},{2,4},{4,6},{6,0},{1,3},{3,5},{5,7},{7,1},{8,10},{10,12},{12... | collective-permute-start | bytes 786440 | tf_op jit(solution)/shard_map/ppermute | solution.py:204
  76.5 16.1 %collective-permute-start.17 = (f32[128,1024]{1,0:T(8,128)S(1)}, f32[128,1024]{1,0:T(8,128)S(1)}, u32[]{:S(2)}, u32[]{:S(2)}) collective-permute-start(f32[128,1024]{1,0:T(8,128)S(1)} %collective-permute-done.10.refs_2_), channel_id=1, source_target_pairs={{0,1},{1,0},{2,3},{3,2},{4,5},{5,4},{6,7},{7,6},{8,9},{9,8},{10,11... | collective-permute-start | bytes 1572872 | tf_op jit(solution)/shard_map/ppermute | solution.py:204
  78.8 13.7 %collective-permute-start.18 = (f32[128,1024]{1,0:T(8,128)S(1)}, f32[128,1024]{1,0:T(8,128)S(1)}, u32[]{:S(2)}, u32[]{:S(2)}) collective-permute-start(f32[128,1024]{1,0:T(8,128)S(1)} %collective-permute-done.13.refs_4_), channel_id=1, source_target_pairs={{0,1},{1,0},{2,3},{3,2},{4,5},{5,4},{6,7},{7,6},{8,9},{9,8},{10,11... | collective-permute-start | bytes 1572872 | tf_op jit(solution)/shard_map/ppermute | solution.py:204
  79.0 8.0 %collective-permute-start.14 = (f32[64,1024]{1,0:T(8,128)S(1)}, f32[64,1024]{1,0:T(8,128)}, u32[]{:S(2)}, u32[]{:S(2)}) collective-permute-start(f32[64,1024]{1,0:T(8,128)S(1)} %slice.26), channel_id=1, source_target_pairs={{0,6},{2,0},{4,2},{6,4},{1,7},{3,1},{5,3},{7,5},{8,14},{10,8},{12,... | collective-permute-start | bytes 786440 | tf_op jit(solution)/shard_map/ppermute | solution.py:204
  83.3 11.5 %collective-permute-start.12 = (f32[64,1024]{1,0:T(8,128)S(1)}, f32[64,1024]{1,0:T(8,128)}, u32[]{:S(2)}, u32[]{:S(2)}) collective-permute-start(f32[64,1024]{1,0:T(8,128)S(1)} %collective-permute-done.11.refs_0_), channel_id=1, source_target_pairs={{0,1},{1,0},{2,3},{3,2},{4,5},{5,4},{6,7},{7,6},{8,9},{9,8},{10,11... | collective-permute-start | bytes 786440 | tf_op jit(solution)/shard_map/ppermute | solution.py:204
  87.0 7.9 %collective-permute-start.15 = (f32[64,1024]{1,0:T(8,128)}, f32[64,1024]{1,0:T(8,128)}, u32[]{:S(2)}, u32[]{:S(2)}) collective-permute-start(f32[64,1024]{1,0:T(8,128)} %collective-permute-done.14.refs_2_), channel_id=1, source_target_pairs={{0,1},{1,0},{2,3},{3,2},{4,5},{5,4},{6,7},{7,6},{8,9},{9,8},{10,11... | collective-permute-start | bytes 786440 | tf_op jit(solution)/shard_map/ppermute | solution.py:204
  (6 other events, 49.8 us)

commit v5 on v4

--- a/solution.py
+++ b/solution.py
@@ -35,7 +35,20 @@
     return master_new, moment_one_new, moment_two_new
 
 
-def state_kernel(tiles, master, one, two, average, master_out, one_out, two_out, average_out):
+def state_kernel(where, tiles, master, one, two, average, *refs):
+    pieces, (master_out, one_out, two_out, average_out, out, sems) = refs[:4], refs[5:]
+    copies = []
+    for n, piece in enumerate(pieces):
+        first = pl.multiple_of(where[n], SUB)
+        copies.append(
+            pltpu.make_async_copy(piece, out.at[pl.ds(first, piece.shape[0])], sems.at[n])
+        )
+
+    @pl.when(pl.program_id(0) == 0)
+    def _():
+        for copy in copies:
+            copy.start()
+
     for unit in range(tiles.shape[1]):
         for half in range(2):
             rows = pl.ds(unit * UNIT + half * SUB, SUB)
@@ -50,8 +63,13 @@
                     average_rate * average[rows, cols] + (1.0 - average_rate) * m
                 )
 
-
-def owner_update(tiles, master, one, two, average):
+    @pl.when(pl.program_id(0) == pl.num_programs(0) - 1)
+    def _():
+        for copy in copies:
+            copy.wait()
+
+
+def owner_update(tiles, master, one, two, average, where, pieces, held):
     rows, width = master.shape
     units = 8
     steps = rows // (units * UNIT)
@@ -59,14 +77,23 @@
     return pl.pallas_call(
         state_kernel,
         grid=(steps,),
-        in_specs=[pl.BlockSpec((N_REP, units, SUB, LANES), lambda s: (0, s, 0, 0))] + [block] * 4,
-        out_specs=[block] * 4,
-        out_shape=[jax.ShapeDtypeStruct((rows, width), jnp.float32)] * 4,
+        in_specs=[
+            pl.BlockSpec(memory_space=pltpu.SMEM),
+            pl.BlockSpec((N_REP, units, SUB, LANES), lambda s: (0, s, 0, 0)),
+        ]
+        + [block] * 4
+        + [pl.BlockSpec(piece.shape, lambda s: (0, 0)) for piece in pieces]
+        + [pl.BlockSpec(memory_space=pl.ANY)],
+        out_specs=[block] * 4 + [pl.BlockSpec(memory_space=pl.ANY)],
+        out_shape=[jax.ShapeDtypeStruct((rows, width), jnp.float32)] * 4
+        + [jax.ShapeDtypeStruct(held.shape, jnp.float32)],
+        scratch_shapes=[pltpu.SemaphoreType.DMA((4,))],
+        input_output_aliases={10: 4},
         cost_estimate=pl.CostEstimate(
             flops=20 * rows * width, bytes_accessed=36 * rows * width, transcendentals=rows * width
         ),
         name="owner_update",
-    )(tiles, master, one, two, average)
+    )(where, tiles, master, one, two, average, *pieces, held)
 
 
 def place_kernel(count, where, *refs):
@@ -220,8 +247,9 @@
             chip = (x + step) % 4
             pieces += [piece, shift(piece, "core", 1)]
             where += [(chip * 2 + core) * rows + offset, (chip * 2 + 1 - core) * rows + offset]
-        out = place(where, pieces, rows * N_SHARD, out)
-    return out
+        if out is None:
+            out = place(where, pieces, rows * N_SHARD)
+    return jnp.stack(where).astype(jnp.int32), pieces, out
 
 
 def local(
@@ -291,7 +319,7 @@
     near = jnp.stack([weights] + [shift(weights, "z", step) for step in (3, 2, 1)])
     far = [near] + [shift(near, "y", step) for step in (3, 2, 1)]
     lines = arrange(jnp.stack([z, y]).astype(jnp.int32), far)
-    new_params = gather_lines(lines)
+    where, pieces, window = gather_lines(lines)
 
     same = jnp.stack([summed] + [shift(summed, "x", step) for step in (3, 2, 1)])
     other = shift(same, "core", 1)
@@ -300,7 +328,9 @@
     index = index * own_units + slot_unit % own_units
     tiles = pick(jnp.where(slot_used, index, -1).astype(jnp.int32), same, other)
     tiles = lax.all_to_all(tiles, REP, split_axis=0, concat_axis=0, tiled=True)
-    outs = owner_update(tiles, master[0], moment_one[0], moment_two[0], average[0])
+    *outs, new_params = owner_update(
+        tiles, master[0], moment_one[0], moment_two[0], average[0], where, pieces, window
+    )
     return (new_params, *(o[None] for o in outs))
 
 

time: 98.1 us -> 97.9 us (level)
  waiting for transfers between devices: 25.4 us -> 27.4 us
  Pallas kernels: 13.7 us -> 12.2 us
    pallas_call x2 -> x1, Pallas kernels: 4.37 us -> 2.25 us  [place(): pl.pallas_call(functools.partial(place_kernel, count), in_specs=[pl.Block...]
    ppermute x23, waiting for transfers between devices: 24.8 us -> 26.8 us  [shift(): lax.ppermute(array, axis, [(i, (i + step) % size) for i in range(size)])]
  transfers between devices with their start and end apart: 25 -> 25, of which waited for: 10 -> 7; matrix products, arithmetic and copies ran while one was open for 5% -> 5% of each run, Pallas kernels for 9% -> 5%
where the time goes in v5:
time: 97.9 us; the launch traced here: 97.5 us
  starting transfers between devices  50.3 us (51%)
  waiting for transfers between devices  27.4 us (28%)
  Pallas kernels  12.2 us (12%)
  local copies, waits for them, and re-layouts  3.58 us (4%)
  other arithmetic  3.02 us (3%)
    ppermute x23, starting transfers between devices, shift(): lax.ppermute(array, axis, [(i, (i + step) % size) for i in range(size)])  34.5 us
    ppermute x23, waiting for transfers between devices, shift(): lax.ppermute(array, axis, [(i, (i + step) % size) for i in range(size)])  26.8 us
    all_to_all x1, starting transfers between devices, local(): lax.all_to_all(packed, ALL, split_axis=0, concat_axis=0, tiled=True)  11.5 us
    pallas_call x1, Pallas kernels, owner_update(): pl.pallas_call(state_kernel, grid=(steps,), in_specs=[pl.BlockSpec(memory...  4.63 us
    all_to_all x1, starting transfers between devices, local(): tiles = lax.all_to_all(tiles, REP, split_axis=0, concat_axis=0, tiled=True)  4.35 us
    pallas_call x1, Pallas kernels, tile_order(): pl.pallas_call(tile_kernel, in_specs=[pl.BlockSpec(memory_space=pl.ANY)],...  2.94 us
    pallas_call x1, Pallas kernels, place(): pl.pallas_call(functools.partial(place_kernel, count), in_specs=[pl.Block...  2.25 us
  transfers between devices with their start and end apart: 25, of which 7 were waited for; matrix products, arithmetic and copies ran while one was open for 5% of the time, Pallas kernels for 5%

profile of v5, /device:TPU:1, one launch (start us, length us, event | category | flops | bytes accessed | tf_op | source)
XLA Modules:
  0.0 97.5 jit_solution(12580818914268450581)
XLA Ops:
  0.6 2.9 %tile_order.1 = bf16[16,64,8,128]{3,2,1,0:T(8,128)(2,1)} custom-call(bf16[64,2,8,1024]{3,2,1,0:T(8,128)(2,1)} %bitcast.93), custom_call_target="tpu_custom_call" | custom-call | bytes 4194304 | tf_op jit(solution)/shard_map/tile_order/pallas_call | solution.py:213
  3.6 11.5 %all-to-all-start = ((bf16[128,8,8,128]{3,2,1,0:T(8,128)(2,1)}), bf16[128,8,8,128]{3,2,1,0:T(8,128)(2,1)S(1)}, u32[]{:S(2)}, u32[]{:S(2)}) async-start(bf16[128,8,8,128]{3,2,1,0:T(8,128)(2,1)} %bitcast.91), calls=%async_computation | async-start | bytes 4194304 | tf_op jit(solution)/shard_map/all_to_all | solution.py:294
  19.0 1.1 %collective-permute-start.4 = (f32[4,8,3,8,128]{4,3,2,1,0:T(8,128)S(1)}, f32[4,8,3,8,128]{4,3,2,1,0:T(8,128)S(1)}, u32[]{:S(2)}, u32[]{:S(2)}) collective-permute-start(f32[4,8,3,8,128]{4,3,2,1,0:T(8,128)S(1)} %dynamic-slice_bitcast_fusion), channel_id=1, source_target_pairs={{0,1},{1,0},{2,3},{3,2},{4,5},{5,4},{6,7},{7,6},{8,9},{9,8},{10,11... | collective-permute-start | bytes 1179656 | tf_op jit(solution)/shard_map/ppermute | solution.py:231
  20.4 1.2 %collective-permute-done.4 = f32[4,8,3,8,128]{4,3,2,1,0:T(8,128)S(1)} collective-permute-done((f32[4,8,3,8,128]{4,3,2,1,0:T(8,128)S(1)}, f32[4,8,3,8,128]{4,3,2,1,0:T(8,128)S(1)}, u32[]{:S(2)}, u32[]{:S(2)}) %collective-permute-start.4) | collective-permute-done | bytes 393248 | tf_op jit(solution)/shard_map/ppermute | solution.py:231
  21.5 1.0 %bitcast_add_fusion = f32[4,8,3,8,128]{4,3,2,1,0:T(8,128)S(1)} fusion(f32[4,8,3,8,128]{4,3,2,1,0:T(8,128)S(1)} %collective-permute-done.4, f32[4,2,8,3,8,128]{5,4,3,2,1,0:T(8,128)} %copy-done, s32[]{:T(128)S(6)} %select_n.197), kind=kLoop, calls=%fused_computation.3 | loop fusion | flops 98304 | bytes 1179652 | tf_op jit(solution)/shard_map/add | solution.py:311
  23.4 2.0 %collective-permute-start.6 = (f32[8,3,8,128]{3,2,0,1:T(8,128)S(1)}, f32[8,3,8,128]{3,2,0,1:T(8,128)S(1)}, u32[]{:S(2)}, u32[]{:S(2)}) collective-permute-start(f32[8,3,8,128]{3,2,0,1:T(8,128)S(1)} %bitcast.103), channel_id=1, source_target_pairs={{0,6},{2,0},{4,2},{6,4},{1,7},{3,1},{5,3},{7,5},{8,14},{10,8},{12,... | collective-permute-start | bytes 294920 | tf_op jit(solution)/shard_map/ppermute | solution.py:231
  26.6 15.8 %collective-permute-done.5 = f32[8,3,8,128]{3,2,0,1:T(8,128)S(1)} collective-permute-done((f32[8,3,8,128]{3,2,0,1:T(8,128)S(1)}, f32[8,3,8,128]{3,2,0,1:T(8,128)S(1)}, u32[]{:S(2)}, u32[]{:S(2)}) %collective-permute-start.5) | collective-permute-done | bytes 98336 | tf_op jit(solution)/shard_map/ppermute | solution.py:231
  42.4 2.4 %collective-permute-done.7 = f32[8,3,8,128]{3,2,0,1:T(8,128)S(1)} collective-permute-done((f32[8,3,8,128]{3,2,0,1:T(8,128)S(1)}, f32[8,3,8,128]{3,2,0,1:T(8,128)S(1)}, u32[]{:S(2)}, u32[]{:S(2)}) %collective-permute-start.7) | collective-permute-done | bytes 98336 | tf_op jit(solution)/shard_map/ppermute | solution.py:231
  46.7 2.9 %collective-permute-start.9 = (f32[8,8,128]{2,1,0:T(8,128)S(1)}, f32[8,8,128]{2,1,0:T(8,128)S(1)}, u32[]{:S(2)}, u32[]{:S(2)}) collective-permute-start(f32[8,8,128]{2,1,0:T(8,128)S(1)} %fusion.15), channel_id=1, source_target_pairs={{0,64},{32,96},{64,0},{96,32},{1,65},{33,97},{65,1},{97,33},{2,66}... | collective-permute-start | bytes 98312 | tf_op jit(solution)/shard_map/ppermute | solution.py:231
  50.9 1.8 %collective-permute-start.1 = (f32[8,8,128]{2,1,0:T(8,128)S(1)}, f32[8,8,128]{2,1,0:T(8,128)S(1)}, u32[]{:S(2)}, u32[]{:S(2)}) collective-permute-start(f32[8,8,128]{2,1,0:T(8,128)S(1)} %convert_reduce_fusion), channel_id=1, source_target_pairs={{0,4},{2,6},{4,0},{6,2},{1,5},{3,7},{5,1},{7,3},{8,12},{10,14},{12... | collective-permute-start | bytes 98312 | tf_op jit(solution)/shard_map/ppermute | solution.py:231
  53.4 1.3 %collective-permute-start.13 = (f32[4,8,8,128]{3,2,1,0:T(8,128)S(1)}, f32[4,8,8,128]{3,2,1,0:T(8,128)S(1)}, u32[]{:S(2)}, u32[]{:S(2)}) collective-permute-start(f32[4,8,8,128]{3,2,1,0:T(8,128)S(1)} %pad_maximum_fusion.2.refs_0_), channel_id=1, source_target_pairs={{0,8},{8,16},{16,24},{24,0},{1,9},{9,17},{17,25},{25,1},{2,10},{10... | collective-permute-start | bytes 393224 | tf_op jit(solution)/shard_map/ppermute | solution.py:231
  54.7 2.5 %collective-permute-start.12 = (f32[4,8,8,128]{3,2,1,0:T(8,128)S(1)}, f32[4,8,8,128]{3,2,1,0:T(8,128)S(1)}, u32[]{:S(2)}, u32[]{:S(2)}) collective-permute-start(f32[4,8,8,128]{3,2,1,0:T(8,128)S(1)} %pad_maximum_fusion.2.refs_0_), channel_id=1, source_target_pairs={{0,16},{8,24},{16,0},{24,8},{1,17},{9,25},{17,1},{25,9},{2,18},{10... | collective-permute-start | bytes 393224 | tf_op jit(solution)/shard_map/ppermute | solution.py:231
  57.3 1.1 %collective-permute-start.11 = (f32[4,8,8,128]{3,2,1,0:T(8,128)S(1)}, f32[4,8,8,128]{3,2,1,0:T(8,128)S(1)}, u32[]{:S(2)}, u32[]{:S(2)}) collective-permute-start(f32[4,8,8,128]{3,2,1,0:T(8,128)S(1)} %pad_maximum_fusion.2.refs_0_), channel_id=1, source_target_pairs={{0,24},{8,0},{16,8},{24,16},{1,25},{9,1},{17,9},{25,17},{2,26},{10... | collective-permute-start | bytes 393224 | tf_op jit(solution)/shard_map/ppermute | solution.py:231
  58.5 3.2 %collective-permute-start.3 = (f32[4,8,8,128]{3,2,1,0:T(8,128)S(1)}, f32[4,8,8,128]{3,2,1,0:T(8,128)S(1)}, u32[]{:S(2)}, u32[]{:S(2)}) collective-permute-start(f32[4,8,8,128]{3,2,1,0:T(8,128)S(1)} %pad_maximum_fusion.1.same), channel_id=1, source_target_pairs={{0,1},{1,0},{2,3},{3,2},{4,5},{5,4},{6,7},{7,6},{8,9},{9,8},{10,11... | collective-permute-start | bytes 393224 | tf_op jit(solution)/shard_map/ppermute | solution.py:231
  62.5 1.0 %collective-permute-start.17 = (f32[128,1024]{1,0:T(8,128)S(1)}, f32[128,1024]{1,0:T(8,128)S(1)}, u32[]{:S(2)}, u32[]{:S(2)}) collective-permute-start(f32[128,1024]{1,0:T(8,128)S(1)} %arrange.1.refs_0_), channel_id=1, source_target_pairs={{0,6},{2,0},{4,2},{6,4},{1,7},{3,1},{5,3},{7,5},{8,14},{10,8},{12,... | collective-permute-start | bytes 1572872 | tf_op jit(solution)/shard_map/ppermute | solution.py:231
  64.1 1.6 %pick.1 = f32[16,16,8,128]{3,2,1,0:T(8,128)} custom-call(s32[16]{0:T(128)S(1)} %fusion.22.index, f32[4,8,8,128]{3,2,1,0:T(8,128)S(1)} %pad_maximum_fusion.1.same, f32[4,8,8,128]{3,2,1,0:T(8,128)S(1)} %collective-permute-done.3.other), custom_call_target="tpu_custom_call" | custom-call | bytes 1048576 | tf_op jit(solution)/shard_map/pick/pallas_call | solution.py:178
  65.8 4.3 %all-to-all-start.1 = ((f32[16,16,8,128]{3,2,1,0:T(8,128)}), f32[16,16,8,128]{3,2,1,0:T(8,128)}, u32[]{:S(2)}, u32[]{:S(2)}) async-start(f32[16,16,8,128]{3,2,1,0:T(8,128)} %pick.1), calls=%async_computation.1 | async-start | bytes 2097152 | tf_op jit(solution)/shard_map/all_to_all | solution.py:330
  70.1 4.7 %collective-permute-start.20 = (f32[128,1024]{1,0:T(8,128)S(1)}, f32[128,1024]{1,0:T(8,128)S(1)}, u32[]{:S(2)}, u32[]{:S(2)}) collective-permute-start(f32[128,1024]{1,0:T(8,128)S(1)} %arrange.1.refs_0_), channel_id=1, source_target_pairs={{0,1},{1,0},{2,3},{3,2},{4,5},{5,4},{6,7},{7,6},{8,9},{9,8},{10,11... | collective-permute-start | bytes 1572872 | tf_op jit(solution)/shard_map/ppermute | solution.py:231
  74.9 2.2 %collective-permute-start.22 = (f32[128,1024]{1,0:T(8,128)S(1)}, f32[128,1024]{1,0:T(8,128)S(1)}, u32[]{:S(2)}, u32[]{:S(2)}) collective-permute-start(f32[128,1024]{1,0:T(8,128)S(1)} %collective-permute-done.17.refs_4_), channel_id=1, source_target_pairs={{0,1},{1,0},{2,3},{3,2},{4,5},{5,4},{6,7},{7,6},{8,9},{9,8},{10,11... | collective-permute-start | bytes 1572872 | tf_op jit(solution)/shard_map/ppermute | solution.py:231
  77.1 2.1 %collective-permute-start.21 = (f32[128,1024]{1,0:T(8,128)S(1)}, f32[128,1024]{1,0:T(8,128)S(1)}, u32[]{:S(2)}, u32[]{:S(2)}) collective-permute-start(f32[128,1024]{1,0:T(8,128)S(1)} %collective-permute-done.14.refs_2_), channel_id=1, source_target_pairs={{0,1},{1,0},{2,3},{3,2},{4,5},{5,4},{6,7},{7,6},{8,9},{9,8},{10,11... | collective-permute-start | bytes 1572872 | tf_op jit(solution)/shard_map/ppermute | solution.py:231
  80.7 6.5 %collective-permute-done.18.refs_2_ = f32[64,1024]{1,0:T(8,128)S(1)} collective-permute-done((f32[64,1024]{1,0:T(8,128)S(1)}, f32[64,1024]{1,0:T(8,128)S(1)}, u32[]{:S(2)}, u32[]{:S(2)}) %collective-permute-start.18) | collective-permute-done | bytes 262176 | tf_op jit(solution)/shard_map/ppermute | solution.py:231
  88.7 1.2 %collective-permute-start.16 = (f32[64,1024]{1,0:T(8,128)}, f32[64,1024]{1,0:T(8,128)}, u32[]{:S(2)}, u32[]{:S(2)}) collective-permute-start(f32[64,1024]{1,0:T(8,128)} %collective-permute-done.15.refs_0_), channel_id=1, source_target_pairs={{0,1},{1,0},{2,3},{3,2},{4,5},{5,4},{6,7},{7,6},{8,9},{9,8},{10,11... | collective-permute-start | bytes 786440 | tf_op jit(solution)/shard_map/ppermute | solution.py:231
  90.5 2.3 %place.1.refs_4_ = f32[1024,1024]{1,0:T(8,128)} custom-call(s32[6]{0:T(128)S(1)} %stack.100.where, f32[128,1024]{1,0:T(8,128)S(1)} %arrange.1.refs_0_, f32[128,1024]{1,0:T(8,128)S(1)} %collective-permute-done.20.refs_1_, f32[128,1024]{1,0:T(8,128)S(1)} %collective-permute-done.14.refs_2_, f32[128,1024]{1,0:T(8,128)S(1)} %collective-permute-done.21.refs_3_, ...), custom_call_target="tpu_custom_call" | custom-call | bytes 6291456 | tf_op jit(solution)/shard_map/place/pallas_call | solution.py:116
  92.8 4.6 %owner_update.1 = (f32[256,1024]{1,0:T(8,128)}, f32[256,1024]{1,0:T(8,128)}, f32[256,1024]{1,0:T(8,128)}, f32[256,1024]{1,0:T(8,128)}, f32[1024,1024]{1,0:T(8,128)}) custom-call(s32[4]{0:T(128)} %pad_add_fusion.where, f32[16,16,8,128]{3,2,1,0:T(8,128)} %all-to-all-done.1.tiles, f32[256,1024]{1,0:T(8,128)} %bitcast.95, ...), custom_call_target="tpu_custom_call", output_to_operand_aliasing={{4}: (10, {})} | custom-call | flops 5242880 | bytes 9437184 | tf_op jit(solution)/shard_map/owner_update/pallas_call | solution.py:77
  (78 shorter events, 15.2 us)
Async XLA Ops:
  3.6 41.8 %all-to-all-start = ((bf16[128,8,8,128]{3,2,1,0:T(8,128)(2,1)}), bf16[128,8,8,128]{3,2,1,0:T(8,128)(2,1)S(1)}, u32[]{:S(2)}, u32[]{:S(2)}) async-start(bf16[128,8,8,128]{3,2,1,0:T(8,128)(2,1)} %bitcast.91), calls=%async_computation | async-start | bytes 4194304 | tf_op jit(solution)/shard_map/all_to_all | solution.py:294
  22.7 19.7 %collective-permute-start.5 = (f32[8,3,8,128]{3,2,0,1:T(8,128)S(1)}, f32[8,3,8,128]{3,2,0,1:T(8,128)S(1)}, u32[]{:S(2)}, u32[]{:S(2)}) collective-permute-start(f32[8,3,8,128]{3,2,0,1:T(8,128)S(1)} %bitcast.104), channel_id=1, source_target_pairs={{0,2},{2,4},{4,6},{6,0},{1,3},{3,5},{5,7},{7,1},{8,10},{10,12},{12... | collective-permute-start | bytes 294920 | tf_op jit(solution)/shard_map/ppermute | solution.py:231
  23.4 19.0 %collective-permute-start.6 = (f32[8,3,8,128]{3,2,0,1:T(8,128)S(1)}, f32[8,3,8,128]{3,2,0,1:T(8,128)S(1)}, u32[]{:S(2)}, u32[]{:S(2)}) collective-permute-start(f32[8,3,8,128]{3,2,0,1:T(8,128)S(1)} %bitcast.103), channel_id=1, source_target_pairs={{0,6},{2,0},{4,2},{6,4},{1,7},{3,1},{5,3},{7,5},{8,14},{10,8},{12,... | collective-permute-start | bytes 294920 | tf_op jit(solution)/shard_map/ppermute | solution.py:231
  25.4 19.4 %collective-permute-start.7 = (f32[8,3,8,128]{3,2,0,1:T(8,128)S(1)}, f32[8,3,8,128]{3,2,0,1:T(8,128)S(1)}, u32[]{:S(2)}, u32[]{:S(2)}) collective-permute-start(f32[8,3,8,128]{3,2,0,1:T(8,128)S(1)} %bitcast.102), channel_id=1, source_target_pairs={{0,4},{2,6},{4,0},{6,2},{1,5},{3,7},{5,1},{7,3},{8,12},{10,14},{12... | collective-permute-start | bytes 294920 | tf_op jit(solution)/shard_map/ppermute | solution.py:231
  45.8 6.8 %collective-permute-start.10 = (f32[8,8,128]{2,1,0:T(8,128)S(1)}, f32[8,8,128]{2,1,0:T(8,128)S(1)}, u32[]{:S(2)}, u32[]{:S(2)}) collective-permute-start(f32[8,8,128]{2,1,0:T(8,128)S(1)} %fusion.15), channel_id=1, source_target_pairs={{0,32},{32,64},{64,96},{96,0},{1,33},{33,65},{65,97},{97,1},{2,34}... | collective-permute-start | bytes 98312 | tf_op jit(solution)/shard_map/ppermute | solution.py:231
  46.7 6.7 %collective-permute-start.9 = (f32[8,8,128]{2,1,0:T(8,128)S(1)}, f32[8,8,128]{2,1,0:T(8,128)S(1)}, u32[]{:S(2)}, u32[]{:S(2)}) collective-permute-start(f32[8,8,128]{2,1,0:T(8,128)S(1)} %fusion.15), channel_id=1, source_target_pairs={{0,64},{32,96},{64,0},{96,32},{1,65},{33,97},{65,1},{97,33},{2,66}... | collective-permute-start | bytes 98312 | tf_op jit(solution)/shard_map/ppermute | solution.py:231
  49.6 3.8 %collective-permute-start.8 = (f32[8,8,128]{2,1,0:T(8,128)S(1)}, f32[8,8,128]{2,1,0:T(8,128)S(1)}, u32[]{:S(2)}, u32[]{:S(2)}) collective-permute-start(f32[8,8,128]{2,1,0:T(8,128)S(1)} %fusion.15), channel_id=1, source_target_pairs={{0,96},{32,0},{64,32},{96,64},{1,97},{33,1},{65,33},{97,65},{2,98}... | collective-permute-start | bytes 98312 | tf_op jit(solution)/shard_map/ppermute | solution.py:231
  50.5 6.7 %collective-permute-start.2 = (f32[8,8,128]{2,1,0:T(8,128)S(1)}, f32[8,8,128]{2,1,0:T(8,128)S(1)}, u32[]{:S(2)}, u32[]{:S(2)}) collective-permute-start(f32[8,8,128]{2,1,0:T(8,128)S(1)} %convert_reduce_fusion), channel_id=1, source_target_pairs={{0,2},{2,4},{4,6},{6,0},{1,3},{3,5},{5,7},{7,1},{8,10},{10,12},{12... | collective-permute-start | bytes 98312 | tf_op jit(solution)/shard_map/ppermute | solution.py:231
  50.9 7.6 %collective-permute-start.1 = (f32[8,8,128]{2,1,0:T(8,128)S(1)}, f32[8,8,128]{2,1,0:T(8,128)S(1)}, u32[]{:S(2)}, u32[]{:S(2)}) collective-permute-start(f32[8,8,128]{2,1,0:T(8,128)S(1)} %convert_reduce_fusion), channel_id=1, source_target_pairs={{0,4},{2,6},{4,0},{6,2},{1,5},{3,7},{5,1},{7,3},{8,12},{10,14},{12... | collective-permute-start | bytes 98312 | tf_op jit(solution)/shard_map/ppermute | solution.py:231
  52.7 5.8 %collective-permute-start = (f32[8,8,128]{2,1,0:T(8,128)S(1)}, f32[8,8,128]{2,1,0:T(8,128)S(1)}, u32[]{:S(2)}, u32[]{:S(2)}) collective-permute-start(f32[8,8,128]{2,1,0:T(8,128)S(1)} %convert_reduce_fusion), channel_id=1, source_target_pairs={{0,6},{2,0},{4,2},{6,4},{1,7},{3,1},{5,3},{7,5},{8,14},{10,8},{12,... | collective-permute-start | bytes 98312 | tf_op jit(solution)/shard_map/ppermute | solution.py:231
  53.4 8.3 %collective-permute-start.13 = (f32[4,8,8,128]{3,2,1,0:T(8,128)S(1)}, f32[4,8,8,128]{3,2,1,0:T(8,128)S(1)}, u32[]{:S(2)}, u32[]{:S(2)}) collective-permute-start(f32[4,8,8,128]{3,2,1,0:T(8,128)S(1)} %pad_maximum_fusion.2.refs_0_), channel_id=1, source_target_pairs={{0,8},{8,16},{16,24},{24,0},{1,9},{9,17},{17,25},{25,1},{2,10},{10... | collective-permute-start | bytes 393224 | tf_op jit(solution)/shard_map/ppermute | solution.py:231
  54.7 6.9 %collective-permute-start.12 = (f32[4,8,8,128]{3,2,1,0:T(8,128)S(1)}, f32[4,8,8,128]{3,2,1,0:T(8,128)S(1)}, u32[]{:S(2)}, u32[]{:S(2)}) collective-permute-start(f32[4,8,8,128]{3,2,1,0:T(8,128)S(1)} %pad_maximum_fusion.2.refs_0_), channel_id=1, source_target_pairs={{0,16},{8,24},{16,0},{24,8},{1,17},{9,25},{17,1},{25,9},{2,18},{10... | collective-permute-start | bytes 393224 | tf_op jit(solution)/shard_map/ppermute | solution.py:231
  57.3 4.5 %collective-permute-start.11 = (f32[4,8,8,128]{3,2,1,0:T(8,128)S(1)}, f32[4,8,8,128]{3,2,1,0:T(8,128)S(1)}, u32[]{:S(2)}, u32[]{:S(2)}) collective-permute-start(f32[4,8,8,128]{3,2,1,0:T(8,128)S(1)} %pad_maximum_fusion.2.refs_0_), channel_id=1, source_target_pairs={{0,24},{8,0},{16,8},{24,16},{1,25},{9,1},{17,9},{25,17},{2,26},{10... | collective-permute-start | bytes 393224 | tf_op jit(solution)/shard_map/ppermute | solution.py:231
  58.5 5.6 %collective-permute-start.3 = (f32[4,8,8,128]{3,2,1,0:T(8,128)S(1)}, f32[4,8,8,128]{3,2,1,0:T(8,128)S(1)}, u32[]{:S(2)}, u32[]{:S(2)}) collective-permute-start(f32[4,8,8,128]{3,2,1,0:T(8,128)S(1)} %pad_maximum_fusion.1.same), channel_id=1, source_target_pairs={{0,1},{1,0},{2,3},{3,2},{4,5},{5,4},{6,7},{7,6},{8,9},{9,8},{10,11... | collective-permute-start | bytes 393224 | tf_op jit(solution)/shard_map/ppermute | solution.py:231
  62.5 12.3 %collective-permute-start.17 = (f32[128,1024]{1,0:T(8,128)S(1)}, f32[128,1024]{1,0:T(8,128)S(1)}, u32[]{:S(2)}, u32[]{:S(2)}) collective-permute-start(f32[128,1024]{1,0:T(8,128)S(1)} %arrange.1.refs_0_), channel_id=1, source_target_pairs={{0,6},{2,0},{4,2},{6,4},{1,7},{3,1},{5,3},{7,5},{8,14},{10,8},{12,... | collective-permute-start | bytes 1572872 | tf_op jit(solution)/shard_map/ppermute | solution.py:231
  63.6 13.5 %collective-permute-start.14 = (f32[128,1024]{1,0:T(8,128)S(1)}, f32[128,1024]{1,0:T(8,128)S(1)}, u32[]{:S(2)}, u32[]{:S(2)}) collective-permute-start(f32[128,1024]{1,0:T(8,128)S(1)} %arrange.1.refs_0_), channel_id=1, source_target_pairs={{0,2},{2,4},{4,6},{6,0},{1,3},{3,5},{5,7},{7,1},{8,10},{10,12},{12... | collective-permute-start | bytes 1572872 | tf_op jit(solution)/shard_map/ppermute | solution.py:231
  65.8 27.0 %all-to-all-start.1 = ((f32[16,16,8,128]{3,2,1,0:T(8,128)}), f32[16,16,8,128]{3,2,1,0:T(8,128)}, u32[]{:S(2)}, u32[]{:S(2)}) async-start(f32[16,16,8,128]{3,2,1,0:T(8,128)} %pick.1), calls=%async_computation.1 | async-start | bytes 2097152 | tf_op jit(solution)/shard_map/all_to_all | solution.py:330
  70.1 20.4 %collective-permute-start.20 = (f32[128,1024]{1,0:T(8,128)S(1)}, f32[128,1024]{1,0:T(8,128)S(1)}, u32[]{:S(2)}, u32[]{:S(2)}) collective-permute-start(f32[128,1024]{1,0:T(8,128)S(1)} %arrange.1.refs_0_), channel_id=1, source_target_pairs={{0,1},{1,0},{2,3},{3,2},{4,5},{5,4},{6,7},{7,6},{8,9},{9,8},{10,11... | collective-permute-start | bytes 1572872 | tf_op jit(solution)/shard_map/ppermute | solution.py:231
  74.9 15.7 %collective-permute-start.22 = (f32[128,1024]{1,0:T(8,128)S(1)}, f32[128,1024]{1,0:T(8,128)S(1)}, u32[]{:S(2)}, u32[]{:S(2)}) collective-permute-start(f32[128,1024]{1,0:T(8,128)S(1)} %collective-permute-done.17.refs_4_), channel_id=1, source_target_pairs={{0,1},{1,0},{2,3},{3,2},{4,5},{5,4},{6,7},{7,6},{8,9},{9,8},{10,11... | collective-permute-start | bytes 1572872 | tf_op jit(solution)/shard_map/ppermute | solution.py:231
  77.1 13.5 %collective-permute-start.21 = (f32[128,1024]{1,0:T(8,128)S(1)}, f32[128,1024]{1,0:T(8,128)S(1)}, u32[]{:S(2)}, u32[]{:S(2)}) collective-permute-start(f32[128,1024]{1,0:T(8,128)S(1)} %collective-permute-done.14.refs_2_), channel_id=1, source_target_pairs={{0,1},{1,0},{2,3},{3,2},{4,5},{5,4},{6,7},{7,6},{8,9},{9,8},{10,11... | collective-permute-start | bytes 1572872 | tf_op jit(solution)/shard_map/ppermute | solution.py:231
  79.1 8.0 %collective-permute-start.18 = (f32[64,1024]{1,0:T(8,128)S(1)}, f32[64,1024]{1,0:T(8,128)S(1)}, u32[]{:S(2)}, u32[]{:S(2)}) collective-permute-start(f32[64,1024]{1,0:T(8,128)S(1)} %slice.26), channel_id=1, source_target_pairs={{0,6},{2,0},{4,2},{6,4},{1,7},{3,1},{5,3},{7,5},{8,14},{10,8},{12,... | collective-permute-start | bytes 786440 | tf_op jit(solution)/shard_map/ppermute | solution.py:231
  79.7 8.9 %collective-permute-start.15 = (f32[64,1024]{1,0:T(8,128)S(1)}, f32[64,1024]{1,0:T(8,128)}, u32[]{:S(2)}, u32[]{:S(2)}) collective-permute-start(f32[64,1024]{1,0:T(8,128)S(1)} %slice.25), channel_id=1, source_target_pairs={{0,2},{2,4},{4,6},{6,0},{1,3},{3,5},{5,7},{7,1},{8,10},{10,12},{12... | collective-permute-start | bytes 786440 | tf_op jit(solution)/shard_map/ppermute | solution.py:231
  87.2 5.6 %collective-permute-start.19 = (f32[64,1024]{1,0:T(8,128)S(1)}, f32[64,1024]{1,0:T(8,128)}, u32[]{:S(2)}, u32[]{:S(2)}) collective-permute-start(f32[64,1024]{1,0:T(8,128)S(1)} %collective-permute-done.18.refs_2_), channel_id=1, source_target_pairs={{0,1},{1,0},{2,3},{3,2},{4,5},{5,4},{6,7},{7,6},{8,9},{9,8},{10,11... | collective-permute-start | bytes 786440 | tf_op jit(solution)/shard_map/ppermute | solution.py:231
  88.7 4.2 %collective-permute-start.16 = (f32[64,1024]{1,0:T(8,128)}, f32[64,1024]{1,0:T(8,128)}, u32[]{:S(2)}, u32[]{:S(2)}) collective-permute-start(f32[64,1024]{1,0:T(8,128)} %collective-permute-done.15.refs_0_), channel_id=1, source_target_pairs={{0,1},{1,0},{2,3},{3,2},{4,5},{5,4},{6,7},{7,6},{8,9},{9,8},{10,11... | collective-permute-start | bytes 786440 | tf_op jit(solution)/shard_map/ppermute | solution.py:231
  (7 other events, 55.4 us)
